TPU v7x, 32 devices: a whole 2x2x4 slice. The times are simulated.
32 devices in a mesh: dp: 8 (over z, y), tensor: 4 (over x, core).
Axes of the slice: x: 2, y: 2, z: 4, core: 2. Of those that a mesh axis runs over, the one named last changes fastest.
Arguments:
- tokens: bfloat16 [4096, 768], P('dp'), may hold values from -6 to 6
- cotangent: bfloat16 [4096, 768], P('dp'), may hold values from -6 to 6
- lengths: int32 [8, 16], P('dp'), may hold values from 0 to 512, as said below
- labels: int32 [8, 16], P('dp'), may hold values from 0 to 2
- w_qkv: bfloat16 [768, 3, 768], P(None, None, 'tensor'), may hold values from -0.21875 to 0.21875
- qv_bias: float32 [2, 768], P(None, 'tensor'), may hold values from -1.5 to 1.5
- w_out: bfloat16 [768, 768], P('tensor'), may hold values from -0.75 to 0.75
- branch_bias: float32 [2, 768], replicated, may hold values from -1.5 to 1.5
- norm_gain: float32 [2, 768], replicated, may hold values from 0.5 to 1.5
- norm_shift: float32 [2, 768], replicated, may hold values from -1.5 to 1.5
- w_up: bfloat16 [768, 3072], P(None, 'tensor'), may hold values from -0.21875 to 0.21875
- up_bias: bfloat16 [3072], P('tensor'), may hold values from -1.5 to 1.5
- w_down: bfloat16 [3072, 768], P('tensor'), may hold values from -0.109375 to 0.109375
- w_pool: bfloat16 [768, 768], replicated, may hold values from -0.21875 to 0.21875
- pool_bias: float32 [768], replicated, may hold values from -1.5 to 1.5
- w_class: bfloat16 [768, 3], replicated, may hold values from -0.625 to 0.625
- class_bias: float32 [3], replicated, may hold values from -2.5 to 2.5
Outputs:
- block_out: bfloat16 [4096, 768], P('dp')
- grad_tokens: bfloat16 [4096, 768], P('dp')
- ramp_loss: float32 [], replicated
- ramp_entropy: float32 [], replicated
- grad_qkv: float32 [768, 3, 768], P('dp', None, 'tensor')
- grad_qv_bias: float32 [2, 768], P(None, ('tensor', 'dp'))
- grad_out: float32 [768, 768], P('tensor', 'dp')
- grad_branch_bias: float32 [2, 768], P(None, 'dp')
- grad_norm_gain: float32 [2, 768], P(None, 'dp')
- grad_norm_shift: float32 [2, 768], P(None, 'dp')
- grad_up: float32 [768, 3072], P('dp', 'tensor')
- grad_up_bias: float32 [3072], P(('tensor', 'dp'))
- grad_down: float32 [3072, 768], P('tensor', 'dp')
- grad_pool: float32 [768, 768], P('dp')
- grad_pool_bias: float32 [768], P('dp')
- grad_class: float32 [768, 3], P('dp')
- grad_class_bias: float32 [3], replicated
Inputs may be any that keep to these rules, and one draw needn't show every extreme that they name: In each packed row the lengths of its items stand in its first slots and the remaining slots hold 0; the first slot is at least 1 and a row's lengths sum to at most 512. Some row of every draw is a single item of 512 tokens.
All inputs are finite; a program needn't handle non-finite values.
Results may differ from a plain program's by a relative error of at most 0.02.
Values may be sent and summed in bfloat16 or wider, within the bound.
A program may use at most 128 MiB of HBM per device.

v0:
```python
from functools import partial

import jax
import jax.numpy as jnp
from jax import lax
from jax.sharding import PartitionSpec as P

HD = 64


masked_score = -1e30
norm_eps = 1e-12


def contract_rows(first_mat, second_mat):
    return lax.dot_general(
        first_mat, second_mat, (((0,), (0,)), ((), ())), preferred_element_type=jnp.float32
    )


def times_transposed(first_mat, second_mat):
    return lax.dot_general(
        first_mat, second_mat, (((1,), (1,)), ((), ())), preferred_element_type=jnp.float32
    )


def segment_table(lengths, row_length):
    end_places = jnp.cumsum(lengths, axis=1, dtype=jnp.int32)
    starts = end_places - lengths
    places = jnp.arange(row_length, dtype=jnp.int32)
    segment = jnp.sum(
        (end_places[:, None, :] <= places[None, :, None]).astype(jnp.int32), axis=2, dtype=jnp.int32
    )
    live_token = (places[None, :] < end_places[:, -1:]).astype(jnp.float32)
    return (segment, live_token, starts)


def norm_forward(values, gain_row, shift_row):
    mean_row = jnp.mean(values, axis=-1, keepdims=True)
    centered = values - mean_row
    inv_scale = lax.rsqrt(jnp.mean(centered * centered, axis=-1, keepdims=True) + norm_eps)
    normed = centered * inv_scale
    return (normed * gain_row + shift_row, normed, inv_scale)


def norm_backward(gradient, normed, inv_scale, gain_row):
    scaled = gradient * gain_row
    inner_term = (
        scaled
        - jnp.mean(scaled, axis=-1, keepdims=True)
        - normed * jnp.mean(scaled * normed, axis=-1, keepdims=True)
    )
    return (inner_term * inv_scale, jnp.sum(gradient * normed, axis=0), jnp.sum(gradient, axis=0))


def gelu_back(pre_act, gradient):
    return jax.vjp(lambda v: jax.nn.gelu(v, approximate=False), pre_act)[1](gradient)[0]


def row_scores(queries, keys_row, segment, head_size):
    raw_scores = jnp.einsum(
        "qhd,khd->hqk", queries, keys_row, preferred_element_type=jnp.float32
    ) * head_size ** (-0.5)
    same_segment = (segment[:, None] == segment[None, :])[None]
    return jnp.where(same_segment, raw_scores, masked_score)


def attend_row(packed, head_count, head_size):
    queries, keys_row, values, segment = packed
    row_length = queries.shape[0]
    queries = queries.reshape(row_length, head_count, head_size)
    keys_row = keys_row.reshape(row_length, head_count, head_size)
    values = values.reshape(row_length, head_count, head_size)
    scores = row_scores(queries, keys_row, segment, head_size)
    row_top = jnp.max(scores, axis=-1, keepdims=True)
    expo_terms = jnp.exp(scores - row_top)
    denominator = jnp.sum(expo_terms, axis=-1, keepdims=True)
    prob_low = (expo_terms / denominator).astype(jnp.bfloat16)
    context = jnp.einsum("hqk,khd->qhd", prob_low, values, preferred_element_type=jnp.float32)
    log_total = (row_top + jnp.log(denominator))[..., 0]
    return (context.reshape(row_length, head_count * head_size).astype(jnp.bfloat16), log_total)


def attend_back(packed, head_count, head_size):
    queries, keys_row, values, segment, log_total, d_context = packed
    row_length = queries.shape[0]
    queries = queries.reshape(row_length, head_count, head_size)
    keys_row = keys_row.reshape(row_length, head_count, head_size)
    values = values.reshape(row_length, head_count, head_size)
    d_context = d_context.reshape(row_length, head_count, head_size)
    scores = row_scores(queries, keys_row, segment, head_size)
    prob_rows = jnp.exp(scores - log_total[..., None])
    d_value = jnp.einsum(
        "hqk,qhd->khd",
        prob_rows.astype(jnp.bfloat16),
        d_context,
        preferred_element_type=jnp.float32,
    )
    d_probs = jnp.einsum("qhd,khd->hqk", d_context, values, preferred_element_type=jnp.float32)
    d_scores = (
        prob_rows * (d_probs - jnp.sum(prob_rows * d_probs, axis=-1, keepdims=True))
    ).astype(jnp.bfloat16)
    d_query = jnp.einsum(
        "hqk,khd->qhd", d_scores, keys_row, preferred_element_type=jnp.float32
    ) * head_size ** (-0.5)
    d_key = jnp.einsum(
        "hqk,qhd->khd", d_scores, queries, preferred_element_type=jnp.float32
    ) * head_size ** (-0.5)
    local_width = head_count * head_size
    joined = jnp.concatenate(
        [
            d_query.reshape(row_length, local_width),
            d_key.reshape(row_length, local_width),
            d_value.reshape(row_length, local_width),
        ],
        axis=1,
    )
    return joined.astype(jnp.bfloat16)


def on_device(
    tokens,
    cotangent,
    lengths,
    labels,
    w_qkv,
    qv_bias,
    w_out,
    branch_bias,
    norm_gain,
    norm_shift,
    w_up,
    up_bias,
    w_down,
    w_pool,
    pool_bias,
    w_class,
    class_bias,
):
    row_count, slot_count = lengths.shape
    token_count, model_width = tokens.shape
    row_length = token_count // row_count
    local_width = w_out.shape[0]
    head_count = local_width // HD
    class_count = w_class.shape[1]
    segment, live_token, starts = segment_table(lengths, row_length)
    item_live = (lengths > 0).astype(jnp.float32).reshape(-1)
    first_index = (
        jnp.arange(row_count, dtype=jnp.int32)[:, None] * row_length
        + jnp.minimum(starts, row_length - 1)
    ).reshape(-1)
    label_hot = (
        labels.reshape(-1)[:, None] == jnp.arange(class_count, dtype=jnp.int32)[None, :]
    ).astype(jnp.float32)
    flat_qkv = w_qkv.reshape(model_width, 3 * local_width)
    qkv_bias = jnp.concatenate([qv_bias[0], jnp.zeros((local_width,), jnp.float32), qv_bias[1]])
    qkv_rows = (jnp.dot(tokens, flat_qkv, preferred_element_type=jnp.float32) + qkv_bias).astype(
        jnp.bfloat16
    )
    queries = qkv_rows[:, :local_width].reshape(row_count, row_length, local_width)
    keys_all = qkv_rows[:, local_width : 2 * local_width].reshape(
        row_count, row_length, local_width
    )
    values = qkv_rows[:, 2 * local_width :].reshape(row_count, row_length, local_width)
    context, log_total = lax.map(
        partial(attend_row, head_count=head_count, head_size=HD),
        (queries, keys_all, values, segment),
    )
    context = context.reshape(token_count, local_width)
    attention = (
        lax.psum(
            jnp.dot(context, w_out, preferred_element_type=jnp.float32).astype(jnp.bfloat16),
            "tensor",
        ).astype(jnp.float32)
        + branch_bias[0]
    )
    hidden, normed_one, scale_one = norm_forward(
        tokens.astype(jnp.float32) + attention, norm_gain[0], norm_shift[0]
    )
    hidden_low = hidden.astype(jnp.bfloat16)
    pre_act = jnp.dot(hidden_low, w_up, preferred_element_type=jnp.float32) + up_bias.astype(
        jnp.float32
    )
    act_low = jax.nn.gelu(pre_act, approximate=False).astype(jnp.bfloat16)
    branch = lax.psum(
        jnp.dot(act_low, w_down, preferred_element_type=jnp.float32).astype(jnp.bfloat16), "tensor"
    )
    output, normed_two, scale_two = norm_forward(
        hidden + (branch.astype(jnp.float32) + branch_bias[1]), norm_gain[1], norm_shift[1]
    )
    picked_low = jnp.take(output, first_index, axis=0).astype(jnp.bfloat16)
    pooled = jnp.tanh(jnp.dot(picked_low, w_pool, preferred_element_type=jnp.float32) + pool_bias)
    pooled_low = pooled.astype(jnp.bfloat16)
    logits = jnp.dot(pooled_low, w_class, preferred_element_type=jnp.float32) + class_bias
    row_top = jnp.max(logits, axis=1, keepdims=True)
    shifted = logits - row_top
    log_probs = shifted - jnp.log(jnp.sum(jnp.exp(shifted), axis=1, keepdims=True))
    class_probs = jnp.exp(log_probs)
    item_ce = -jnp.sum(label_hot * log_probs, axis=1) * item_live
    item_ent = -jnp.sum(class_probs * log_probs, axis=1) * item_live
    local_totals = jnp.stack([jnp.sum(item_live), jnp.sum(item_ce), jnp.sum(item_ent)])
    class_totals = jnp.stack(
        [
            jnp.sum(class_probs * item_live[:, None], axis=0),
            jnp.sum(label_hot * item_live[:, None], axis=0),
        ]
    )
    totals, class_sums = lax.psum((local_totals, class_totals), "dp")
    item_count = totals[0]
    ramp_loss = totals[1] / item_count
    ramp_entropy = totals[2] / item_count
    d_logits = (class_probs - label_hot) * (item_live / item_count)[:, None]
    grad_class = lax.dot_general(
        pooled_low.astype(jnp.float32),
        d_logits,
        (((0,), (0,)), ((), ())),
        precision=lax.Precision.HIGHEST,
        preferred_element_type=jnp.float32,
    )
    grad_class_bias = (class_sums[0] - class_sums[1]) / item_count
    d_pooled = lax.dot_general(
        d_logits,
        w_class.astype(jnp.float32),
        (((1,), (1,)), ((), ())),
        precision=lax.Precision.HIGHEST,
        preferred_element_type=jnp.float32,
    )
    d_pre = (d_pooled * (1.0 - pooled * pooled)).astype(jnp.bfloat16)
    grad_pool = contract_rows(picked_low, d_pre)
    grad_pool_bias = jnp.sum(d_pre.astype(jnp.float32), axis=0)
    d_picked = times_transposed(d_pre, w_pool)
    d_output = cotangent.astype(jnp.float32) * live_token.reshape(-1)[:, None]
    d_output = d_output.at[first_index].add(d_picked)
    d_second, gain_two, shift_two = norm_backward(d_output, normed_two, scale_two, norm_gain[1])
    d_branch = d_second.astype(jnp.bfloat16)
    bias_two = jnp.sum(d_second, axis=0)
    grad_down = contract_rows(act_low, d_branch)
    d_act = times_transposed(d_branch, w_down)
    d_pre_act = gelu_back(pre_act, d_act).astype(jnp.bfloat16)
    grad_up = contract_rows(hidden_low, d_pre_act)
    grad_up_bias = jnp.sum(d_pre_act.astype(jnp.float32), axis=0)
    d_hidden = lax.psum(times_transposed(d_pre_act, w_up).astype(jnp.bfloat16), "tensor").astype(
        jnp.float32
    )
    d_first, gain_one, shift_one = norm_backward(
        d_hidden + d_second, normed_one, scale_one, norm_gain[0]
    )
    d_att = d_first.astype(jnp.bfloat16)
    bias_one = jnp.sum(d_first, axis=0)
    grad_out = contract_rows(context, d_att)
    d_context = times_transposed(d_att, w_out).astype(jnp.bfloat16)
    d_qkv = lax.map(
        partial(attend_back, head_count=head_count, head_size=HD),
        (
            queries,
            keys_all,
            values,
            segment,
            log_total,
            d_context.reshape(row_count, row_length, local_width),
        ),
    )
    d_qkv = d_qkv.reshape(token_count, 3 * local_width)
    grad_qkv = contract_rows(tokens, d_qkv).reshape(model_width, 3, local_width)
    d_qkv_wide = d_qkv.astype(jnp.float32)
    grad_qv = jnp.stack(
        [
            jnp.sum(d_qkv_wide[:, :local_width], axis=0),
            jnp.sum(d_qkv_wide[:, 2 * local_width :], axis=0),
        ]
    )
    d_tokens = (
        lax.psum(times_transposed(d_qkv, flat_qkv).astype(jnp.bfloat16), "tensor").astype(
            jnp.float32
        )
        + d_first
    )
    grad_tokens = d_tokens.astype(jnp.bfloat16)
    vectors = jnp.stack(
        [bias_one, bias_two, gain_one, gain_two, shift_one, shift_two, grad_pool_bias]
    )
    summed = (
        lax.psum_scatter(
            grad_qkv.astype(jnp.bfloat16), "dp", scatter_dimension=0, tiled=True
        ).astype(jnp.float32),
        lax.psum_scatter(
            grad_qv.astype(jnp.bfloat16), "dp", scatter_dimension=1, tiled=True
        ).astype(jnp.float32),
        lax.psum_scatter(
            grad_out.astype(jnp.bfloat16), "dp", scatter_dimension=1, tiled=True
        ).astype(jnp.float32),
        lax.psum_scatter(
            vectors.astype(jnp.bfloat16), "dp", scatter_dimension=1, tiled=True
        ).astype(jnp.float32),
        lax.psum_scatter(
            grad_up.astype(jnp.bfloat16), "dp", scatter_dimension=0, tiled=True
        ).astype(jnp.float32),
        lax.psum_scatter(
            grad_up_bias.astype(jnp.bfloat16), "dp", scatter_dimension=0, tiled=True
        ).astype(jnp.float32),
        lax.psum_scatter(
            grad_down.astype(jnp.bfloat16), "dp", scatter_dimension=1, tiled=True
        ).astype(jnp.float32),
        lax.psum_scatter(
            grad_pool.astype(jnp.bfloat16), "dp", scatter_dimension=0, tiled=True
        ).astype(jnp.float32),
        lax.psum_scatter(
            grad_class.astype(jnp.bfloat16), "dp", scatter_dimension=0, tiled=True
        ).astype(jnp.float32),
    )
    vector_share = summed[3]
    return (
        output.astype(jnp.bfloat16),
        grad_tokens,
        ramp_loss,
        ramp_entropy,
        summed[0],
        summed[1],
        summed[2],
        vector_share[0:2],
        vector_share[2:4],
        vector_share[4:6],
        summed[4],
        summed[5],
        summed[6],
        summed[7],
        vector_share[6],
        summed[8],
        grad_class_bias,
    )


def solution(mesh):
    in_specs = (
        P("dp", None),
        P("dp", None),
        P("dp", None),
        P("dp", None),
        P(None, None, "tensor"),
        P(None, "tensor"),
        P("tensor", None),
        P(),
        P(),
        P(),
        P(None, "tensor"),
        P("tensor"),
        P("tensor", None),
        P(),
        P(),
        P(),
        P(),
    )
    out_specs = (
        P("dp", None),
        P("dp", None),
        P(),
        P(),
        P("dp", None, "tensor"),
        P(None, ("tensor", "dp")),
        P("tensor", "dp"),
        P(None, "dp"),
        P(None, "dp"),
        P(None, "dp"),
        P("dp", "tensor"),
        P(("tensor", "dp")),
        P("tensor", "dp"),
        P("dp", None),
        P("dp"),
        P("dp", None),
        P(),
    )
    return jax.shard_map(
        on_device, mesh=mesh, in_specs=in_specs, out_specs=out_specs, check_vma=False
    )
```

profile of v0, /device:TPU:0, one launch (start us, length us, event | category | flops | bytes accessed | tf_op | source)
XLA Modules:
  0.0 696.1 jit_solution(5936897519087431770)
XLA Ops:
  9.3 2.1 fusion.13
  20.9 33.2 %all-reduce.9.cloned.1.call-done = bf16[512,768]{1,0:T(8,128)(2,1)} async-done(((bf16[512,768]{1,0:T(8,128)(2,1)}), bf16[512,768]{1,0:T(8,128)(2,1)}) %all-reduce.9.cloned.1.call-update) | async-done | bytes 786448 | tf_op jit(solution)/shard_map/psum | solution.py:171
  54.1 1.5 fusion.14
  56.2 5.5 multiply_convert_fusion.1
  62.6 1.7 convolution_convert_fusion.5
  65.4 33.7 %all-reduce.11.cloned.1.call-done = bf16[512,768]{1,0:T(8,128)(2,1)} async-done(((bf16[512,768]{1,0:T(8,128)(2,1)}), bf16[512,768]{1,0:T(8,128)(2,1)}) %all-reduce.11.cloned.1.call-update) | async-done | bytes 786448 | tf_op jit(solution)/shard_map/psum | solution.py:185
  99.1 2.1 fusion.50
  103.4 2.6 gather_fusion
  105.9 1.7 fusion.21
  112.4 2.5 pad_maximum_fusion.4
  114.9 2.1 convert_multiply_fusion
  117.0 22.0 %all-reduce.2 = (f32[3]{0:T(128)}, f32[2,3]{1,0:T(2,128)}) all-reduce(f32[3]{0:T(128)} %pad_maximum_fusion.4, f32[2,3]{1,0:T(2,128)} %pad_maximum_fusion.3), channel_id=1, replica_groups=mesh['dp'=8,'tensor'=4] {'dp'}, use_global_device_ids=true, to_apply=%region_17.18 | all-reduce | flops 9 | bytes 72 | tf_op jit(solution)/shard_map/psum | solution.py:208
  139.0 1.4 fusion.55
  142.2 1.6 fusion.59
  144.4 2.3 fusion.60
  146.8 3.5 scatter_fusion
  150.3 2.8 multiply_reduce_fusion.1
  155.9 1.8 fusion.58
  158.7 1.7 convolution_convert_fusion.4
  164.8 1.6 convolution_convert_fusion.10
  166.4 1.5 copy.59
  168.0 23.5 %all-reduce.13.cloned.1.call-done = bf16[512,768]{1,0:T(8,128)(2,1)} async-done(((bf16[512,768]{1,0:T(8,128)(2,1)}), bf16[512,768]{1,0:T(8,128)(2,1)}) %all-reduce.13.cloned.1.call-update) | async-done | bytes 786448 | tf_op jit(solution)/shard_map/psum | solution.py:242
  191.5 2.5 multiply_reduce_fusion.2
  196.7 1.3 fusion.18
  204.3 1.4 stack.79
  205.7 1.6 copy.57
  207.3 3.2 convolution_convert_fusion.6
  210.5 2.6 convolution_convert_fusion.8
  213.1 1.9 copy.55
  215.1 2.7 convolution_convert_fusion.3
  217.8 2.3 copy.48
  220.2 3.1 convolution_convert_fusion
  223.4 3.5 convolution_convert_fusion.1
  227.0 1.6 convolution_convert_fusion.2
  234.5 21.3 %reduce-scatter.27.cloned.1.call-done = bf16[96,3]{1,0:T(8,128)(2,1)} async-done(((bf16[768,3]{1,0:T(8,128)(2,1)}), bf16[96,3]{1,0:T(8,128)(2,1)}) %reduce-scatter.27.cloned.1.call-update) | async-done | bytes 592
  257.5 19.5 %all-reduce.3 = (bf16[2,192]{1,0:T(2,128)(2,1)S(1)}, bf16[768]{0:T(1024)(128)(2,1)S(1)}) all-reduce(bf16[2,192]{1,0:T(2,128)(2,1)S(1)} %pad_maximum_fusion.2, bf16[768]{0:T(1024)(128)(2,1)S(1)} %copy-done.52), channel_id=3, replica_groups=mesh['dp'=8,'tensor'=4] {'dp'}, use_global_device_ids=true, to_apply=%region_29.30.clone | all-reduce | flops 1152 | bytes 4608
  278.3 40.7 %reduce-scatter.25.cloned.1.call-done = bf16[96,7]{1,0:T(8,128)(2,1)} async-done(((bf16[768,7]{1,0:T(8,128)(2,1)}), bf16[96,7]{1,0:T(8,128)(2,1)}) %reduce-scatter.25.cloned.1.call-update) | async-done | bytes 1360
  320.9 34.6 %all-reduce.15.cloned.1.call-done = bf16[512,768]{1,0:T(8,128)(2,1)} async-done(((bf16[512,768]{1,0:T(8,128)(2,1)}), bf16[512,768]{1,0:T(8,128)(2,1)}) %all-reduce.15.cloned.1.call-update) | async-done | bytes 786448 | tf_op jit(solution)/shard_map/psum | solution.py:273
  355.5 2.2 add_convert_fusion
  357.7 62.5 %reduce-scatter.23.cloned.1.call-done = bf16[96,192]{1,0:T(8,128)(2,1)} async-done(((bf16[768,192]{1,0:T(8,128)(2,1)}), bf16[96,192]{1,0:T(8,128)(2,1)}) %reduce-scatter.23.cloned.1.call-update) | async-done | bytes 36880
  421.7 64.8 %reduce-scatter.15.cloned.1.call-done = bf16[96,3,192]{2,0,1:T(8,128)(2,1)} async-done(((bf16[768,3,192]{2,0,1:T(8,128)(2,1)}), bf16[96,3,192]{2,0,1:T(8,128)(2,1)}) %reduce-scatter.15.cloned.1.call-update) | async-done | bytes 110608 | tf_op jit(solution)/shard_map/reduce_scatter | solution.py:283
  486.5 1.6 convert_element_type.218
  488.1 64.8 %reduce-scatter.19.cloned.1.call-done = bf16[768,96]{0,1:T(8,128)(2,1)} async-done(((bf16[768,768]{0,1:T(8,128)(2,1)}), bf16[768,96]{0,1:T(8,128)(2,1)}) %reduce-scatter.19.cloned.1.call-update) | async-done | bytes 147472 | tf_op jit(solution)/shard_map/reduce_scatter | solution.py:301
  553.0 1.6 convert_element_type.229
  554.6 64.6 %reduce-scatter.17.cloned.1.call-done = bf16[96,768]{1,0:T(8,128)(2,1)} async-done(((bf16[768,768]{1,0:T(8,128)(2,1)}), bf16[96,768]{1,0:T(8,128)(2,1)}) %reduce-scatter.17.cloned.1.call-update) | async-done | bytes 147472 | tf_op jit(solution)/shard_map/reduce_scatter | solution.py:295
  619.2 1.6 convert_element_type.226
  620.9 64.8 %reduce-scatter.21.cloned.1.call-done = bf16[96,768]{1,0:T(8,128)(2,1)} async-done(((bf16[768,768]{1,0:T(8,128)(2,1)}), bf16[96,768]{1,0:T(8,128)(2,1)}) %reduce-scatter.21.cloned.1.call-update) | async-done | bytes 147472 | tf_op jit(solution)/shard_map/reduce_scatter | solution.py:304
  685.7 1.6 convert_element_type.231
  (219 shorter events, 48.8 us)
Async XLA Ops:
  7.2 49.0 %copy-start = (bf16[768,768]{1,0:T(8,128)(2,1)S(1)}, bf16[768,768]{1,0:T(8,128)(2,1)}, u32[]{:S(2)}) copy-start(bf16[768,768]{1,0:T(8,128)(2,1)} %param.27) | copy-start | bytes 3538948
  7.2 46.9 %all-reduce.9.cloned.1.call-start = ((), (), s32[]{:S(2)}) async-start(), calls=%async_computation.7 | async-start | bytes 1572864 | tf_op jit(solution)/shard_map/psum | solution.py:171
  14.6 4.5 copy-start.51
  14.6 5.1 copy-start.46
  14.7 5.7 copy-start.47
  14.7 5.7 copy-start.48
  14.7 39.4 %copy-start.7 = (bf16[512,768]{1,0:T(8,128)(2,1)S(1)}, bf16[512,768]{1,0:T(8,128)(2,1)}, u32[]{:S(2)}) copy-start(bf16[512,768]{1,0:T(8,128)(2,1)} %param.17) | copy-start | bytes 2359300
  16.6 82.5 %all-reduce.11.cloned.1.call-start = ((), (), s32[]{:S(2)}) async-start(), calls=%async_computation.8 | async-start | bytes 1572864 | tf_op jit(solution)/shard_map/psum | solution.py:185
  17.9 2.5 copy-start.54
  20.9 35.2 %copy-start.42 = (f32[768]{0:T(1024)}, f32[768]{0:T(1024)S(1)}, u32[]{:S(2)}) copy-start(f32[768]{0:T(1024)S(1)} %get-tuple-element.76) | copy-start | bytes 9220
  55.7 43.5 %copy-start.31 = (f32[512]{0:T(512)}, f32[512]{0:T(512)S(1)}, u32[]{:S(2)}) copy-start(f32[512]{0:T(512)S(1)} %broadcast_multiply_fusion.5) | copy-start | bytes 6148
  56.1 5.6 copy-start.34
  56.2 6.4 copy-start.57
  64.3 127.2 %all-reduce.13.cloned.1.call-start = ((), (), s32[]{:S(2)}) async-start(), calls=%async_computation.9 | async-start | bytes 1572864 | tf_op jit(solution)/shard_map/psum | solution.py:242
  105.9 9.0 %copy-start.22 = (bf16[512,768]{1,0:T(8,128)(2,1)S(1)}, bf16[512,768]{1,0:T(8,128)(2,1)}, u32[]{:S(2)}) copy-start(bf16[512,768]{1,0:T(8,128)(2,1)} %param.18) | copy-start | bytes 2359300
  150.3 2.8 copy-start.10
  150.3 2.8 copy-start.38
  153.1 2.3 copy-start.61
  153.1 2.8 copy-start.62
  153.6 4.1 copy-start.3
  158.7 32.9 %copy-start.4 = (f32[512,768]{1,0:T(8,128)S(1)}, f32[512,768]{1,0:T(8,128)}, u32[]{:S(2)}) copy-start(f32[512,768]{1,0:T(8,128)} %copy-done.3) | copy-start | bytes 4718596
  160.4 95.4 %reduce-scatter.27.cloned.1.call-start = ((), (), s32[]{:S(2)}) async-start(), calls=%async_computation.17 | async-start | bytes 221184
  168.0 151.0 %reduce-scatter.25.cloned.1.call-start = ((), (), s32[]{:S(2)}) async-start(), calls=%async_computation.16 | async-start | bytes 221184
  191.5 2.6 copy-start.9
  191.5 2.6 copy-start.11
  191.5 2.6 copy-start.32
  191.5 2.6 copy-start.35
  194.1 2.5 copy-start.2
  194.9 3.0 copy-start.5
  199.6 4.7 copy-start.43
  199.6 4.7 copy-start.44
  207.2 148.3 %all-reduce.15.cloned.1.call-start = ((), (), s32[]{:S(2)}) async-start(), calls=%async_computation.10 | async-start | bytes 1572864 | tf_op jit(solution)/shard_map/psum | solution.py:273
  210.5 209.7 %reduce-scatter.23.cloned.1.call-start = ((), (), s32[]{:S(2)}) async-start(), calls=%async_computation.15 | async-start | bytes 442368
  215.0 271.4 %reduce-scatter.15.cloned.1.call-start = ((), (), s32[]{:S(2)}) async-start(), calls=%async_computation.11 | async-start | bytes 1327104 | tf_op jit(solution)/shard_map/reduce_scatter | solution.py:283
  220.1 3.2 copy-start.33
  220.2 3.2 copy-start.36
  220.2 332.8 %reduce-scatter.19.cloned.1.call-start = ((), (), s32[]{:S(2)}) async-start(), calls=%async_computation.13 | async-start | bytes 1327104 | tf_op jit(solution)/shard_map/reduce_scatter | solution.py:301
  223.3 3.7 copy-start.27
  223.3 3.7 copy-start.29
  223.3 3.7 copy-start.50
  223.3 395.9 %reduce-scatter.17.cloned.1.call-start = ((), (), s32[]{:S(2)}) async-start(), calls=%async_computation.12 | async-start | bytes 1327104 | tf_op jit(solution)/shard_map/reduce_scatter | solution.py:295
  226.9 6.4 copy-start.55
  226.9 30.3 %copy-start.21 = (bf16[3,64,512]{2,1,0:T(8,128)(2,1)S(1)}, bf16[3,64,512]{2,1,0:T(8,128)(2,1)}, u32[]{:S(2)}) copy-start(bf16[3,64,512]{2,1,0:T(8,128)(2,1)} %fusion.18) | copy-start | bytes 589828
  226.9 30.3 %copy-start.24 = (bf16[3,64,512]{2,1,0:T(8,128)(2,1)S(1)}, bf16[3,64,512]{2,1,0:T(8,128)(2,1)}, u32[]{:S(2)}) copy-start(bf16[3,64,512]{2,1,0:T(8,128)(2,1)} %fusion.16) | copy-start | bytes 589828
  226.9 30.3 %copy-start.25 = (bf16[3,64,512]{2,1,0:T(8,128)(2,1)S(1)}, bf16[3,64,512]{2,1,0:T(8,128)(2,1)}, u32[]{:S(2)}) copy-start(bf16[3,64,512]{2,1,0:T(8,128)(2,1)} %fusion.15) | copy-start | bytes 589828
  226.9 458.7 %reduce-scatter.21.cloned.1.call-start = ((), (), s32[]{:S(2)}) async-start(), calls=%async_computation.14 | async-start | bytes 1327104 | tf_op jit(solution)/shard_map/reduce_scatter | solution.py:304
  228.7 28.8 %copy-start.52 = (bf16[768]{0:T(1024)(128)(2,1)S(1)}, bf16[768]{0:T(1024)(128)(2,1)}, u32[]{:S(2)}) copy-start(bf16[768]{0:T(1024)(128)(2,1)} %get-tuple-element.113) | copy-start | bytes 4612
  228.7 126.8 %copy-start.6 = (f32[512,768]{1,0:T(8,128)S(1)}, f32[512,768]{1,0:T(8,128)}, u32[]{:S(2)}) copy-start(f32[512,768]{1,0:T(8,128)} %copy-done.5) | copy-start | bytes 4718596
  (26 other events, 29.1 us)
Sparse Core Ops, SparseCore 0:
  16.7 37.3 all-reduce.8
  64.4 34.6 all-reduce.10
  160.5 30.9 all-reduce.12
  194.6 61.0 reduce-scatter.26
  258.9 60.0 reduce-scatter.24
  321.8 33.6 all-reduce.14
  358.8 61.3 reduce-scatter.22
  423.5 62.8 reduce-scatter.14
  489.9 63.0 reduce-scatter.18
  556.2 62.9 reduce-scatter.16
  622.6 63.0 reduce-scatter.20
where the time goes:
time: 698 us; the launch traced here: 696 us
  waiting for transfers between devices  509 us (73%)
  matrix products  45 us (6%)
  other arithmetic  43.9 us (6%)
  blocking collectives  41.5 us (6%)
  local copies, waits for them, and re-layouts  35.8 us (5%)
  between operations  20.8 us (3%)
    unnamed x14, waiting for transfers between devices  125 us
    reduce_scatter x1, waiting for transfers between devices, on_device(): lax.psum_scatter(grad_pool.astype(jnp.bfloat16), 'dp', scatter_dimension=...  64.8 us
    reduce_scatter x1, waiting for transfers between devices, on_device(): lax.psum_scatter(grad_down.astype(jnp.bfloat16), 'dp', scatter_dimension=...  64.8 us
    reduce_scatter x1, waiting for transfers between devices, on_device(): lax.psum_scatter(grad_qkv.astype(jnp.bfloat16), 'dp', scatter_dimension=0...  64.8 us
    reduce_scatter x1, waiting for transfers between devices, on_device(): lax.psum_scatter(grad_up.astype(jnp.bfloat16), 'dp', scatter_dimension=0,...  64.6 us
    psum x1, waiting for transfers between devices, on_device(): lax.psum(times_transposed(d_qkv, flat_qkv).astype(jnp.bfloat16), 'tensor')  34.6 us
    psum x1, waiting for transfers between devices, on_device(): lax.psum(jnp.dot(act_low, w_down, preferred_element_type=jnp.float32).ast...  33.7 us
    psum x1, waiting for transfers between devices, on_device(): lax.psum(jnp.dot(context, w_out, preferred_element_type=jnp.float32).asty...  33.2 us
  transfers between devices with their start and end apart: 11, of which 11 were waited for; matrix products, arithmetic and copies ran while one was open for 9% of the time, Pallas kernels for 0%

commit v1 on v0

v1 whole, which is shorter than its diff:
```python
from functools import partial

import jax
import jax.numpy as jnp
from jax import lax
from jax.experimental import pallas as pl
from jax.experimental.pallas import tpu as pltpu
from jax.sharding import PartitionSpec as P

HD = 64
MESH = pl.DeviceIdType.MESH
F32 = jnp.float32
BF16 = jnp.bfloat16
masked_score = -1e30
norm_eps = 1e-12
SQRT_HALF = 0.7071067811865476
PDF_SCALE = 0.3989422804014327
VEC_ROWS = 16


def dot_nn(a, b):
    return lax.dot_general(a, b, (((1,), (0,)), ((), ())), preferred_element_type=F32)


def dot_nt(a, b):
    return lax.dot_general(a, b, (((1,), (1,)), ((), ())), preferred_element_type=F32)


def dot_tn(a, b):
    return lax.dot_general(a, b, (((0,), (0,)), ((), ())), preferred_element_type=F32)


def row_mean(v):
    return jnp.sum(v, axis=1, keepdims=True) * (1.0 / v.shape[1])


def col_sum(v):
    return jnp.sum(v, axis=0, keepdims=True)


def norm_forward(values):
    centered = values - row_mean(values)
    inv_scale = lax.rsqrt(row_mean(centered * centered) + norm_eps)
    return centered * inv_scale, inv_scale


def norm_backward(gradient, normed, inv_scale, gain_row):
    scaled = gradient * gain_row
    inner = scaled - row_mean(scaled) - normed * row_mean(scaled * normed)
    return inner * inv_scale


def gelu_parts(pre_act):
    cdf = 0.5 * (1.0 + lax.erf(pre_act * SQRT_HALF))
    pdf = PDF_SCALE * jnp.exp(-0.5 * pre_act * pre_act)
    return pre_act * cdf, cdf + pre_act * pdf


class Copies:
    def __init__(self, send_sems, recv_sems):
        self.send_sems, self.recv_sems, self.used, self.open = send_sems, recv_sems, 0, []

    def start(self, src, dst, device):
        copy = pltpu.make_async_remote_copy(
            src_ref=src,
            dst_ref=dst,
            send_sem=self.send_sems.at[self.used],
            recv_sem=self.recv_sems.at[self.used],
            device_id=device,
            device_id_type=MESH,
        )
        self.used += 1
        copy.start()
        self.open.append(copy)
        return copy

    def finish(self):
        for copy in self.open:
            copy.wait_send()


class Loads:
    def __init__(self, sems):
        self.sems, self.used = sems, 0

    def start(self, src, dst):
        copy = pltpu.make_async_copy(src, dst, self.sems.at[self.used])
        self.used += 1
        copy.start()
        return copy


def remote_copy_count(groups):
    return 48 + 3 * (1 + 2 * groups) + 8 * groups


def layer_kernel(
    n_dp,
    tok_hbm,
    cot_hbm,
    len_ref,
    lab_ref,
    wqkv_hbm,
    qvb_ref,
    wout_hbm,
    bb_ref,
    ng_ref,
    ns_ref,
    wup_hbm,
    upb_ref,
    wdn_hbm,
    wpool_hbm,
    pb_ref,
    wcls_ref,
    cb_ref,
    bout_hbm,
    gtok_hbm,
    gqkvo_hbm,
    gup_hbm,
    gdn_hbm,
    gpool_hbm,
    vec_hbm,
    tok,
    cot,
    wt,
    wo,
    wup,
    wdn,
    wpool,
    small,
    bias_mask,
    k_nt,
    v_nt,
    k_tr,
    v_tr,
    q_tr,
    probs,
    ctx_all,
    hid,
    hid_low,
    hid_tr,
    tok_tr,
    n_one,
    n_two,
    scale_one,
    scale_two,
    act_low,
    d_gelu,
    acc,
    parts,
    parts_b,
    parts_c,
    out_low,
    d_sec,
    d_br,
    d_br_tr,
    d_pre_low,
    d_first,
    d_att,
    d_att_tr,
    d_ctx,
    d_kv_f32,
    d_kv_send,
    d_kv_recv,
    d_qkv,
    gt_low,
    g_send,
    g_recv,
    g_own,
    y_send,
    y_recv,
    z_send,
    z_recv,
    g_fin,
    pool_fin,
    items,
    items_c,
    picked_t,
    vec,
    vec_c,
    vec_s,
    vec_y,
    vec_z,
    vec_fin,
    cnt,
    cnt_y,
    cnt_s,
    cnt_z,
    load_sems,
    send_sems,
    recv_sems,
):
    groups = n_dp // 2
    dp = lax.axis_index("dp")
    me = lax.axis_index("tensor")
    x = me // 2
    c = lax.rem(me, 2)
    y = lax.rem(dp, 2)
    h = dp // 2
    core_dev = (dp, me + 1 - 2 * c)
    x_dev = (dp, 2 * (1 - x) + c)
    y_dev = (dp + 1 - 2 * y, me)

    def z_dev(k):
        return (lax.rem(h + k, groups) * 2 + y, me)

    token_count, width = tok.shape
    half = token_count // 2
    local_width = wo.shape[1]
    chip_width = 2 * local_width
    heads = chip_width // HD
    slots = len_ref.shape[1]
    shard = width // n_dp
    chunk = 128
    chunks = half // chunk
    tile = 256
    tiles = width // tile
    own_rows = pl.ds(pl.multiple_of(c * half, half), half)

    barrier = pltpu.get_barrier_semaphore()
    peers = [core_dev, x_dev, y_dev] + [z_dev(k) for k in range(1, groups)]
    for peer in peers:
        pl.semaphore_signal(barrier, inc=1, device_id=peer, device_id_type=MESH)

    loads = Loads(load_sems)
    remote = Copies(send_sems, recv_sems)
    load_tok = loads.start(tok_hbm, tok)
    load_wt = loads.start(wqkv_hbm, wt.at[c])
    load_wo = loads.start(wout_hbm, wo.at[me])
    load_wup = loads.start(wup_hbm, wup.at[c])
    load_wdn = loads.start(wdn_hbm, wdn.at[c])
    load_cot = loads.start(cot_hbm.at[own_rows], cot)
    load_pool = loads.start(wpool_hbm, wpool)

    lengths = [len_ref[0, i] for i in range(slots)]
    ends, total = [], 0
    for i in range(slots):
        total = total + lengths[i]
        ends.append(total)
    firsts = [jnp.minimum(ends[i] - lengths[i], token_count - 1) for i in range(slots)]
    key_place = lax.broadcasted_iota(jnp.int32, (token_count, 128), 0)
    query_place = lax.broadcasted_iota(jnp.int32, (8, half), 1) + c * half
    key_segment = jnp.zeros((token_count, 128), jnp.int32)
    query_segment = jnp.zeros((8, half), jnp.int32)
    for i in range(slots):
        key_segment = key_segment + (key_place >= ends[i]).astype(jnp.int32)
        query_segment = query_segment + (query_place >= ends[i]).astype(jnp.int32)
    for n in range(half // 128):
        cols = slice(n * 128, (n + 1) * 128)
        bias_mask[:, cols] = jnp.where(key_segment == query_segment[0:1, cols], 0.0, masked_score)
    item_row = lax.broadcasted_iota(jnp.int32, (slots, 128), 0)
    first_col = jnp.zeros((slots, 128), jnp.int32)
    len_col = jnp.zeros((slots, 128), jnp.int32)
    lab_col = jnp.zeros((slots, 128), jnp.int32)
    for i in range(slots):
        first_col = first_col + jnp.where(item_row == i, firsts[i], 0)
        len_col = len_col + jnp.where(item_row == i, lengths[i], 0)
        lab_col = lab_col + jnp.where(item_row == i, lab_ref[0, i], 0)
    live_all = jnp.where(len_col > 0, 1.0, 0.0)
    cnt[...] = jnp.broadcast_to(col_sum(live_all), cnt.shape)

    small[c] = jnp.concatenate(
        [
            upb_ref[...].astype(F32),
            jnp.concatenate([qvb_ref[...], jnp.zeros((2, width - local_width), F32)], axis=1),
            jnp.zeros((5, width), F32),
        ],
        axis=0,
    )
    vec[...] = jnp.zeros_like(vec)

    pl.semaphore_wait(barrier, len(peers))
    send_wt = remote.start(wqkv_hbm, wt.at[c], core_dev)
    send_small = remote.start(small.at[c], small.at[c], core_dev)
    send_wo_x = remote.start(wout_hbm, wo.at[me], x_dev)
    send_wo_c = remote.start(wout_hbm, wo.at[me], core_dev)
    send_cnt_y = remote.start(cnt, cnt_y, y_dev)
    send_wup = remote.start(wup_hbm, wup.at[c], core_dev)
    send_wdn = remote.start(wdn_hbm, wdn.at[c], core_dev)

    load_tok.wait()
    load_wt.wait()
    send_wt.wait_recv()
    send_small.wait_recv()

    def chip_rows(part):
        rows = slice(part * local_width, (part + 1) * local_width)
        return jnp.concatenate([wt[0, rows, :], wt[1, rows, :]], axis=0)

    def bias_row(part):
        return jnp.concatenate(
            [small[0, 1 + part : 2 + part, :local_width], small[1, 1 + part : 2 + part, :local_width]], axis=1
        )

    def bias_cols(part, columns):
        block = jnp.transpose(jnp.broadcast_to(bias_row(part), (128, chip_width)))
        return jnp.concatenate([block] * (columns // 128), axis=1)

    weights_q, weights_k, weights_v = chip_rows(0), chip_rows(1), chip_rows(2)
    q_tr[...] = (dot_nt(weights_q, tok[own_rows, :]) + bias_cols(0, half)).astype(BF16)
    k_nt[...] = dot_nt(tok[...], weights_k).astype(BF16)
    v_tr[...] = (dot_nt(weights_v, tok[...]) + bias_cols(1, token_count)).astype(BF16)

    half_row = lax.broadcasted_iota(jnp.int32, (128, half), 0) < HD
    inv_root = HD ** (-0.5)

    def half_of(block, side):
        zero = jnp.zeros_like(block)
        return jnp.where(half_row, block, zero) if side == 0 else jnp.where(half_row, zero, block)

    send_ctx = []
    for pair in range(heads // 2):
        pair_rows = slice(pair * 128, (pair + 1) * 128)
        for side in range(2):
            head = 2 * pair + side
            head_rows = slice(head * HD, (head + 1) * HD)
            scores = dot_nn(k_nt[:, pair_rows], half_of(q_tr[pair_rows, :], side)) * inv_root + bias_mask[...]
            terms = jnp.exp(scores - jnp.max(scores, axis=0, keepdims=True))
            weights = terms * (1.0 / col_sum(terms))
            probs[head] = weights
            ctx_all[x, head_rows, :] = dot_nn(v_tr[head_rows, :], weights.astype(BF16)).astype(BF16)
        send_ctx.append(remote.start(ctx_all.at[x, pair_rows], ctx_all.at[x, pair_rows], x_dev))
        if pair == 0:
            send_wo_x.wait_recv()
            other = 2 * (1 - x) + c
            send_wo_f = remote.start(wo.at[other], wo.at[other], core_dev)
            send_cnt_y.wait_recv()
            cnt_s[...] = cnt[...] + cnt_y[...]
            send_cnt_z = [remote.start(cnt_s, cnt_z.at[k - 1], z_dev(k)) for k in range(1, groups)]

    k_tr[...] = dot_nt(weights_k, tok[...]).astype(BF16)
    v_nt[...] = (dot_nt(tok[...], weights_v) + bias_row(1)).astype(BF16)
    tok_tr[...] = jnp.transpose(tok[own_rows, :])

    load_wo.wait()
    send_wo_c.wait_recv()
    send_wo_f.wait_recv()
    for copy in send_ctx:
        copy.wait_recv()

    for i in range(chunks):
        rows = slice(i * chunk, (i + 1) * chunk)
        attention = None
        for g in range(4):
            group_rows = slice((g % 2) * local_width, (g % 2 + 1) * local_width)
            piece = dot_tn(ctx_all[g // 2, group_rows, rows], wo[g]).astype(BF16).astype(F32)
            attention = piece if attention is None else attention + piece
        token_rows = pl.ds(pl.multiple_of(c * half + i * chunk, chunk), chunk)
        normed, inv_scale = norm_forward(tok[token_rows, :].astype(F32) + (attention + bb_ref[0:1, :]))
        n_one[rows, :] = normed
        scale_one[rows, :] = inv_scale
        value = normed * ng_ref[0:1, :] + ns_ref[0:1, :]
        hid[rows, :] = value
        hid_low[rows, :] = value.astype(BF16)

    load_wup.wait()
    load_wdn.wait()
    send_part = []
    for i in range(chunks):
        rows = slice(i * chunk, (i + 1) * chunk)
        for b in range(2):
            core = c if b == 0 else 1 - c
            if i == 0 and b == 1:
                send_wup.wait_recv()
            for n in range(tiles):
                cols = slice(n * tile, (n + 1) * tile)
                pre_act = dot_nn(hid_low[rows, :], wup[core, :, cols]) + small[core, 0:1, cols]
                value, slope = gelu_parts(pre_act)
                act_low[b, rows, cols] = value.astype(BF16)
                d_gelu[b, rows, cols] = slope
            if i == 0 and b == 1:
                send_wdn.wait_recv()
            product = dot_nn(act_low[b, rows, :], wdn[core])
            if b == 0:
                acc[...] = product
            else:
                parts[x, rows, :] = (acc[...] + product).astype(BF16)
        send_part.append(remote.start(parts.at[x, rows], parts.at[x, rows], x_dev))

    hid_tr[...] = jnp.transpose(hid_low[...])
    for k in range(groups - 1):
        send_cnt_z[k].wait_recv()
    item_count = cnt_s[...]
    for k in range(groups - 1):
        item_count = item_count + cnt_z[k]
    inv_count = 1.0 / item_count[0:1, 0:1]

    local_first = first_col[:, 0:1] - c * half
    picked = jnp.zeros((slots, width), F32)
    for i in range(chunks):
        rows = slice(i * chunk, (i + 1) * chunk)
        send_part[i].wait_recv()
        branch = parts[0, rows, :].astype(F32) + parts[1, rows, :].astype(F32)
        normed, inv_scale = norm_forward(hid[rows, :] + (branch + bb_ref[1:2, :]))
        n_two[rows, :] = normed
        scale_two[rows, :] = inv_scale
        low = (normed * ng_ref[1:2, :] + ns_ref[1:2, :]).astype(BF16)
        out_low[rows, :] = low
        places = lax.broadcasted_iota(jnp.int32, (slots, chunk), 1) + i * chunk
        picked = picked + dot_nn((places == local_first).astype(F32).astype(BF16), low)
    send_out = remote.start(out_low, bout_hbm.at[own_rows], core_dev)
    store_out = loads.start(out_low, bout_hbm.at[own_rows])

    load_pool.wait()
    picked_low = picked.astype(BF16)
    pooled = jnp.tanh(dot_nn(picked_low, wpool[...]) + pb_ref[...])
    pooled_low = pooled.astype(BF16)
    classes = wcls_ref.shape[0]
    class_rows = wcls_ref[...].astype(F32)
    class_pad = jnp.concatenate([class_rows, jnp.zeros((16 - classes, width), F32)], axis=0)
    class_lane = lax.broadcasted_iota(jnp.int32, (slots, 16), 1)
    class_bias = jnp.zeros((slots, 16), F32)
    for k in range(classes):
        class_bias = class_bias + jnp.where(class_lane == k, cb_ref[0, k], 0.0)
    logits = jnp.where(class_lane < classes, dot_nt(pooled_low, class_pad.astype(BF16)) + class_bias, masked_score)
    shifted = logits - jnp.max(logits, axis=1, keepdims=True)
    log_probs = shifted - jnp.log(jnp.sum(jnp.exp(shifted), axis=1, keepdims=True))
    class_probs = jnp.exp(log_probs)
    label_hot = jnp.where(class_lane == lab_col[:, 0:1], 1.0, 0.0)
    owned = jnp.where((local_first >= 0) & (local_first < half), live_all[:, 0:1], 0.0)
    item_ce = -jnp.sum(label_hot * log_probs, axis=1, keepdims=True) * owned
    item_ent = -jnp.sum(class_probs * log_probs, axis=1, keepdims=True) * owned
    d_logits = (class_probs - label_hot) * (owned * inv_count)
    d_pooled = jnp.zeros((slots, width), F32)
    for k in range(classes):
        d_pooled = d_pooled + d_logits[:, k : k + 1] * class_rows[k : k + 1, :]
        vec[7 + k : 8 + k, :] = col_sum(d_logits[:, k : k + 1] * pooled_low.astype(F32))
    d_pre = (d_pooled * (1.0 - pooled * pooled)).astype(BF16)
    vec[6:7, :] = col_sum(d_pre.astype(F32))
    lane = lax.broadcasted_iota(jnp.int32, (1, 128), 1)
    vec[10:11, 0:128] = jnp.where(lane == 0, col_sum(item_ce), 0.0) + jnp.where(lane == 1, col_sum(item_ent), 0.0)
    vec[10:11, 128:144] = col_sum(d_logits)
    items[0] = picked_low
    items[1] = d_pre
    send_items = remote.start(items, items_c, core_dev)
    d_picked = dot_nt(d_pre, wpool[...])
    d_high = d_picked.astype(BF16)
    d_both = jnp.concatenate([d_high, (d_picked - d_high.astype(F32)).astype(BF16)], axis=0)
    lane_item = lax.broadcasted_iota(jnp.int32, (1, 2 * slots), 1)
    first_row = jnp.zeros((1, 2 * slots), jnp.int32)
    for i in range(slots):
        first_row = first_row + jnp.where((lane_item == i) | (lane_item == i + slots), firsts[i], 0)

    load_cot.wait()
    gain_two = shift_two = bias_two = None
    up_sums = [[None] * tiles, [None] * tiles]
    send_part_b = []
    for i in range(chunks):
        rows = slice(i * chunk, (i + 1) * chunk)
        places = lax.broadcasted_iota(jnp.int32, (chunk, 2 * slots), 0) + (c * half + i * chunk)
        spread = dot_nn((places == first_row).astype(F32).astype(BF16), d_both)
        token_place = lax.broadcasted_iota(jnp.int32, (chunk, 1), 0) + (c * half + i * chunk)
        live = jnp.where(token_place < total, 1.0, 0.0)
        d_output = cot[rows, :].astype(F32) * live + spread
        normed = n_two[rows, :]
        gain_sum, shift_sum = col_sum(d_output * normed), col_sum(d_output)
        d_second = norm_backward(d_output, normed, scale_two[rows, :], ng_ref[1:2, :])
        bias_sum = col_sum(d_second)
        gain_two = gain_sum if i == 0 else gain_two + gain_sum
        shift_two = shift_sum if i == 0 else shift_two + shift_sum
        bias_two = bias_sum if i == 0 else bias_two + bias_sum
        d_sec[rows, :] = d_second
        d_br[rows, :] = d_second.astype(BF16)
        for b in range(2):
            core = c if b == 0 else 1 - c
            for n in range(tiles):
                cols = slice(n * tile, (n + 1) * tile)
                d_act = dot_nt(d_br[rows, :], wdn[core, cols, :])
                low = (d_act * d_gelu[b, rows, cols]).astype(BF16)
                d_pre_low[b, rows, cols] = low
                up_sum = col_sum(low.astype(F32))
                up_sums[b][n] = up_sum if i == 0 else up_sums[b][n] + up_sum
            product = dot_nt(d_pre_low[b, rows, :], wup[core])
            if b == 0:
                acc[...] = product
            else:
                parts_b[x, rows, :] = (acc[...] + product).astype(BF16)
        send_part_b.append(remote.start(parts_b.at[x, rows], parts_b.at[x, rows], x_dev))
    vec[1:2, :] = bias_two
    vec[3:4, :] = gain_two
    vec[5:6, :] = shift_two
    vec[pl.ds(11 + c, 1), :] = jnp.concatenate(up_sums[0], axis=1)
    vec[pl.ds(12 - c, 1), :] = jnp.concatenate(up_sums[1], axis=1)

    def place_blocks(store, product_of):
        for n in range(tiles):
            cols = slice(n * tile, (n + 1) * tile)
            product = product_of(cols)
            for j in range(n_dp):
                store(j % 2, j // 2, cols, product[j * shard : (j + 1) * shard, :])

    def fill_send(block, product_of):
        def store(low_index, high_index, cols, value):
            g_send[block, low_index, high_index, :, cols] = value.astype(BF16)

        place_blocks(store, product_of)
        return remote.start(g_send.at[block], g_recv.at[block], core_dev)

    def fill_own(block, product_of):
        def store(low_index, high_index, cols, value):
            g_own[block, low_index, high_index, :, cols] = value

        place_blocks(store, product_of)

    def start_y(block, core_copy):
        core_copy.wait_recv()
        copies = []
        for k in list(range(1, groups)) + [0]:
            other = lax.rem(h + k, groups)
            y_send[block, k] = (g_own[block, 1 - y, other] + g_recv[block, 1 - y, other].astype(F32)).astype(BF16)
            copies.append(remote.start(y_send.at[block, k], y_recv.at[block, k], y_dev))
        return copies

    def own_y_sum(block, k):
        other = lax.rem(h + k, groups)
        return (
            g_own[block, y, other] + g_recv[block, y, other].astype(F32) + y_recv[block, k].astype(F32)
        )

    def start_z(block, k, copy):
        copy.wait_recv()
        z_send[block, k - 1] = own_y_sum(block, k).astype(BF16)
        return remote.start(z_send.at[block, k - 1], z_recv.at[block, k - 1], z_dev(k))

    def finish_z(block, y_copies, z_copies, out):
        y_copies[groups - 1].wait_recv()
        result = own_y_sum(block, 0)
        for k in range(1, groups):
            z_copies[k - 1].wait_recv()
            result = result + z_recv[block, k - 1].astype(F32)
        g_fin[block] = result
        return loads.start(g_fin.at[block], out)

    DOWN, UP, QKVO = 0, 1, 2
    d_br_tr[...] = jnp.transpose(d_br[...])
    core_down = fill_send(DOWN, lambda cols: dot_nn(d_br_tr[...], act_low[1, :, cols]))
    core_up = fill_send(UP, lambda cols: dot_nn(hid_tr[...], d_pre_low[1, :, cols]))
    fill_own(DOWN, lambda cols: dot_nn(d_br_tr[...], act_low[0, :, cols]))
    y_down = start_y(DOWN, core_down)
    fill_own(UP, lambda cols: dot_nn(hid_tr[...], d_pre_low[0, :, cols]))
    y_up = start_y(UP, core_up)

    send_items.wait_recv()
    item_slots = (h * 2 + y) * slots
    own_items = pl.ds(pl.multiple_of(item_slots, slots), slots)
    for part in range(2):
        picked_t[part, own_items, :] = items[part] + items_c[part]
    send_items_y = [
        remote.start(picked_t.at[part, own_items], picked_t.at[part, own_items], y_dev) for part in range(2)
    ]

    gain_one = shift_one = bias_one = None
    for i in range(chunks):
        rows = slice(i * chunk, (i + 1) * chunk)
        send_part_b[i].wait_recv()
        d_hidden = parts_b[0, rows, :].astype(F32) + parts_b[1, rows, :].astype(F32) + d_sec[rows, :]
        normed = n_one[rows, :]
        gain_sum, shift_sum = col_sum(d_hidden * normed), col_sum(d_hidden)
        gradient = norm_backward(d_hidden, normed, scale_one[rows, :], ng_ref[0:1, :])
        bias_sum = col_sum(gradient)
        gain_one = gain_sum if i == 0 else gain_one + gain_sum
        shift_one = shift_sum if i == 0 else shift_one + shift_sum
        bias_one = bias_sum if i == 0 else bias_one + bias_sum
        d_first[rows, :] = gradient
        d_att[rows, :] = gradient.astype(BF16)
    vec[0:1, :] = bias_one
    vec[2:3, :] = gain_one
    vec[4:5, :] = shift_one

    chip_out = jnp.concatenate([wo[2 * x], wo[2 * x + 1]], axis=0)
    d_ctx[...] = dot_nt(chip_out, d_att[...]).astype(BF16)
    d_att_tr[...] = jnp.transpose(d_att[...])

    for pair in range(heads // 2):
        pair_rows = slice(pair * 128, (pair + 1) * 128)
        for side in range(2):
            head = 2 * pair + side
            head_rows = slice(head * HD, (head + 1) * HD)
            core, place = head // (heads // 2), (head % (heads // 2)) * HD
            d_probs = dot_nn(v_nt[:, pair_rows], half_of(d_ctx[pair_rows, :], side))
            weights = probs[head]
            delta = col_sum(weights * d_probs)
            d_scores = (weights * (d_probs - delta)).astype(BF16)
            d_value = dot_nt(d_ctx[head_rows, :], weights.astype(BF16))
            d_key = dot_nt(q_tr[head_rows, :], d_scores) * inv_root
            d_query = dot_nn(k_tr[head_rows, :], d_scores) * inv_root
            d_qkv[core, place : place + HD, :] = d_query.astype(BF16)
            for part, value in ((0, d_key), (1, d_value)):
                part_rows = slice(part * local_width + place, part * local_width + place + HD)
                for side_half in range(2):
                    lanes = slice(side_half * half, (side_half + 1) * half)
                    d_kv_f32[side_half, core, part_rows, :] = value[:, lanes]
                    d_kv_send[side_half, core, part_rows, :] = value[:, lanes].astype(BF16)
    send_kv = remote.start(d_kv_send.at[1 - c], d_kv_recv, core_dev)

    z_down = [start_z(DOWN, k, y_down[k - 1]) for k in range(1, groups)]
    for part in range(2):
        send_items_y[part].wait_recv()
    both_items = pl.ds(pl.multiple_of(h * 2 * slots, 2 * slots), 2 * slots)
    send_items_z = [
        remote.start(picked_t.at[part, both_items], picked_t.at[part, both_items], z_dev(k))
        for k in range(1, groups)
        for part in range(2)
    ]

    send_kv.wait_recv()
    for core in range(2):
        d_qkv[core, local_width:, :] = (d_kv_f32[c, core] + d_kv_recv[core].astype(F32)).astype(BF16)

    send_part_c = []
    for i in range(chunks):
        rows = slice(i * chunk, (i + 1) * chunk)
        partial_sum = dot_tn(d_qkv[0, :, rows], wt[0]) + dot_tn(d_qkv[1, :, rows], wt[1])
        parts_c[x, rows, :] = partial_sum.astype(BF16)
        send_part_c.append(remote.start(parts_c.at[x, rows], parts_c.at[x, rows], x_dev))

    def fill_qkvo(core, out, dtype):
        context_rows = pl.ds(pl.multiple_of(core * local_width, local_width), local_width)
        first_part = dot_nt(tok_tr[...], d_qkv[core])
        second_part = dot_nt(d_att_tr[...], ctx_all[x, context_rows, :])
        both = jnp.concatenate([first_part, second_part], axis=1).astype(dtype)
        for j in range(n_dp):
            out[QKVO, j % 2, j // 2] = both[j * shard : (j + 1) * shard, :]

    fill_qkvo(1 - c, g_send, BF16)
    core_qkvo = remote.start(g_send.at[QKVO], g_recv.at[QKVO], core_dev)
    fill_qkvo(c, g_own, F32)
    ones = jnp.ones((8, half), BF16)
    sums = [dot_nt(ones, d_qkv[core])[0:1, :] for core in range(2)]
    vec[13:14, :] = jnp.concatenate(
        [s[:, :local_width] for s in sums] + [s[:, 2 * local_width :] for s in sums], axis=1
    )
    send_vec = remote.start(vec, vec_c, core_dev)
    y_qkvo = start_y(QKVO, core_qkvo)
    send_vec.wait_recv()
    vec_s[...] = vec[...] + vec_c[...]
    send_vec_y = remote.start(vec_s, vec_y, y_dev)

    z_up = [start_z(UP, k, y_up[k - 1]) for k in range(1, groups)]

    for i in range(chunks):
        rows = slice(i * chunk, (i + 1) * chunk)
        send_part_c[i].wait_recv()
        total_grad = parts_c[0, rows, :].astype(F32) + parts_c[1, rows, :].astype(F32) + d_first[rows, :]
        gt_low[rows, :] = total_grad.astype(BF16)
    send_gt = remote.start(gt_low, gtok_hbm.at[own_rows], core_dev)
    store_gt = loads.start(gt_low, gtok_hbm.at[own_rows])

    for copy in send_items_z:
        copy.wait_recv()
    pool_all = dot_tn(picked_t[0], picked_t[1])
    pool_fin[...] = pool_all
    store_pool = loads.start(pool_fin.at[pl.ds(pl.multiple_of(dp * shard, 8), shard)], gpool_hbm)

    store_down = finish_z(DOWN, y_down, z_down, gdn_hbm)
    send_vec_y.wait_recv()
    vec_z[h] = vec_s[...] + vec_y[...]
    send_vec_z = [remote.start(vec_z.at[h], vec_z.at[h], z_dev(k)) for k in range(1, groups)]
    z_qkvo = [start_z(QKVO, k, y_qkvo[k - 1]) for k in range(1, groups)]
    store_up = finish_z(UP, y_up, z_up, gup_hbm)
    for copy in send_vec_z:
        copy.wait_recv()
    vec_total = vec_z[0]
    for k in range(1, groups):
        vec_total = vec_total + vec_z[k]
    vec_fin[...] = vec_total
    vec_fin[14:15, 0:128] = item_count[0:1, :]
    store_vec = loads.start(vec_fin, vec_hbm)
    store_qkvo = finish_z(QKVO, y_qkvo, z_qkvo, gqkvo_hbm)

    send_out.wait_recv()
    send_gt.wait_recv()
    for store in (store_out, store_gt, store_pool, store_down, store_up, store_vec, store_qkvo):
        store.wait()
    remote.finish()


def place_kernel(
    n_dp,
    bout_in,
    gtok_in,
    gqkvo_in,
    gup_in,
    gdn_in,
    gpool_in,
    vec_in,
    bout,
    gtok,
    loss,
    entropy,
    gqkv,
    gqv,
    gout,
    gbranch,
    ggain,
    gshift,
    gup,
    gupb,
    gdn,
    gpool,
    gpoolb,
    gclass,
    gclassb,
    sems,
):
    copies = []
    for i, (src, dst) in enumerate(
        ((bout_in, bout), (gtok_in, gtok), (gup_in, gup), (gdn_in, gdn), (gpool_in, gpool))
    ):
        copy = pltpu.make_async_copy(src, dst, sems.at[i])
        copy.start()
        copies.append(copy)
    dp = lax.axis_index("dp")
    c = lax.rem(lax.axis_index("tensor"), 2)
    width = vec_in.shape[1]
    shard = width // n_dp
    local_width = gout.shape[0]
    for part in range(3):
        gqkv[part] = gqkvo_in[:, part * local_width : (part + 1) * local_width]
    gout[...] = jnp.transpose(gqkvo_in[:, 3 * local_width :])
    sums = vec_in[...]
    mine = pltpu.roll(sums, lax.rem(width - dp * shard, width), axis=1)
    gbranch[...] = mine[0:2, :shard]
    ggain[...] = mine[2:4, :shard]
    gshift[...] = mine[4:6, :shard]
    gpoolb[...] = mine[6:7, :shard]
    gclass[...] = mine[7 : 7 + gclass.shape[0], :shard]
    gupb[...] = jnp.where(c == 0, mine[11:12, :shard], mine[12:13, :shard])
    small = local_width // n_dp
    quarter = pltpu.roll(sums, lax.rem(width - (c * local_width + dp * small), width), axis=1)
    gqv[0:1, :] = quarter[13:14, :small]
    gqv[1:2, :] = quarter[13:14, 2 * local_width : 2 * local_width + small]
    inv_count = 1.0 / sums[14:15, 0:1]
    loss[...] = sums[10:11, 0:1] * inv_count
    entropy[...] = sums[10:11, 1:2] * inv_count
    gclassb[...] = sums[10:11, 128 : 128 + gclassb.shape[1]]
    for copy in copies:
        copy.wait()


def on_device(
    n_dp,
    tokens,
    cotangent,
    lengths,
    labels,
    w_qkv,
    qv_bias,
    w_out,
    branch_bias,
    norm_gain,
    norm_shift,
    w_up,
    up_bias,
    w_down,
    w_pool,
    pool_bias,
    w_class,
    class_bias,
):
    token_count, width = tokens.shape
    local_width = w_out.shape[0]
    chip_width = 2 * local_width
    hidden = w_up.shape[1]
    classes = w_class.shape[1]
    slots = lengths.shape[1]
    groups = n_dp // 2
    shard = width // n_dp
    half = token_count // 2
    heads = chip_width // HD
    assert hidden == width and 4 * local_width == width and lengths.shape[0] == 1
    shape = jax.ShapeDtypeStruct
    anywhere = pl.BlockSpec(memory_space=pl.ANY)
    vmem = pl.BlockSpec(memory_space=pltpu.VMEM)
    smem = pl.BlockSpec(memory_space=pltpu.SMEM)
    block = (2, groups, shard, width)
    copies = remote_copy_count(groups)
    V = pltpu.VMEM
    scratch = [
        V((token_count, width), BF16),
        V((half, width), BF16),
        V((2, 3 * local_width, width), BF16),
        V((4, local_width, width), BF16),
        V((2, width, hidden), BF16),
        V((2, hidden, width), BF16),
        V((width, width), BF16),
        V((2, 8, width), F32),
        V((token_count, half), F32),
        V((token_count, chip_width), BF16),
        V((token_count, chip_width), BF16),
        V((chip_width, token_count), BF16),
        V((chip_width, token_count), BF16),
        V((chip_width, half), BF16),
        V((heads, token_count, half), F32),
        V((2, chip_width, half), BF16),
        V((half, width), F32),
        V((half, width), BF16),
        V((width, half), BF16),
        V((width, half), BF16),
        V((half, width), F32),
        V((half, width), F32),
        V((half, 1), F32),
        V((half, 1), F32),
        V((2, half, hidden), BF16),
        V((2, half, hidden), F32),
        V((128, width), F32),
        V((2, half, width), BF16),
        V((2, half, width), BF16),
        V((2, half, width), BF16),
        V((half, width), BF16),
        V((half, width), F32),
        V((half, width), BF16),
        V((width, half), BF16),
        V((2, half, hidden), BF16),
        V((half, width), F32),
        V((half, width), BF16),
        V((width, half), BF16),
        V((chip_width, half), BF16),
        V((2, 2, 2 * local_width, half), F32),
        V((2, 2, 2 * local_width, half), BF16),
        V((2, 2 * local_width, half), BF16),
        V((2, 3 * local_width, half), BF16),
        V((half, width), BF16),
        V((3,) + block, BF16),
        V((3,) + block, BF16),
        V((3,) + block, F32),
        V((3, groups, shard, width), BF16),
        V((3, groups, shard, width), BF16),
        V((3, groups - 1, shard, width), BF16),
        V((3, groups - 1, shard, width), BF16),
        V((3, shard, width), F32),
        V((width, width), F32),
        V((2, slots, width), BF16),
        V((2, slots, width), BF16),
        V((2, n_dp * slots, width), BF16),
        V((VEC_ROWS, width), F32),
        V((VEC_ROWS, width), F32),
        V((VEC_ROWS, width), F32),
        V((VEC_ROWS, width), F32),
        V((groups, VEC_ROWS, width), F32),
        V((VEC_ROWS, width), F32),
        V((8, 128), F32),
        V((8, 128), F32),
        V((8, 128), F32),
        V((groups - 1, 8, 128), F32),
        pltpu.SemaphoreType.DMA((20,)),
        pltpu.SemaphoreType.DMA((copies,)),
        pltpu.SemaphoreType.DMA((copies,)),
    ]
    found = pl.pallas_call(
        partial(layer_kernel, n_dp),
        out_shape=[
            shape((token_count, width), BF16),
            shape((token_count, width), BF16),
            shape((shard, width), F32),
            shape((shard, width), F32),
            shape((shard, width), F32),
            shape((shard, width), F32),
            shape((VEC_ROWS, width), F32),
        ],
        in_specs=[
            anywhere,
            anywhere,
            smem,
            smem,
            anywhere,
            vmem,
            anywhere,
            vmem,
            vmem,
            vmem,
            anywhere,
            vmem,
            anywhere,
            anywhere,
            vmem,
            vmem,
            smem,
        ],
        out_specs=[anywhere] * 7,
        scratch_shapes=scratch,
        compiler_params=pltpu.CompilerParams(
            collective_id=0, has_side_effects=True, vmem_limit_bytes=62 * 1024 * 1024
        ),
        name="layer",
    )(
        tokens,
        cotangent,
        lengths,
        labels,
        jnp.transpose(w_qkv, (1, 2, 0)).reshape(3 * local_width, width),
        qv_bias,
        w_out,
        branch_bias,
        norm_gain,
        norm_shift,
        w_up,
        up_bias.reshape(1, hidden),
        w_down,
        w_pool,
        pool_bias.reshape(1, width),
        w_class.T,
        class_bias.reshape(1, classes),
    )
    small = local_width // n_dp
    placed = pl.pallas_call(
        partial(place_kernel, n_dp),
        out_shape=[
            shape((token_count, width), BF16),
            shape((token_count, width), BF16),
            shape((1, 1), F32),
            shape((1, 1), F32),
            shape((3, shard, local_width), F32),
            shape((2, small), F32),
            shape((local_width, shard), F32),
            shape((2, shard), F32),
            shape((2, shard), F32),
            shape((2, shard), F32),
            shape((shard, hidden), F32),
            shape((1, hidden // n_dp), F32),
            shape((shard, hidden), F32),
            shape((shard, width), F32),
            shape((1, shard), F32),
            shape((classes, shard), F32),
            shape((1, classes), F32),
        ],
        in_specs=[anywhere, anywhere, vmem, anywhere, anywhere, anywhere, vmem],
        out_specs=[anywhere] * 2 + [vmem] * 8 + [anywhere, vmem, anywhere, anywhere] + [vmem] * 3,
        scratch_shapes=[pltpu.SemaphoreType.DMA((5,))],
        name="place",
    )(*found)
    (
        block_out,
        grad_tokens,
        loss,
        entropy,
        grad_qkv,
        grad_qv,
        grad_out,
        grad_branch,
        grad_gain,
        grad_shift,
        grad_up,
        grad_upb,
        grad_down,
        grad_pool,
        grad_poolb,
        grad_class,
        grad_classb,
    ) = placed
    return (
        block_out,
        grad_tokens,
        loss.reshape(()),
        entropy.reshape(()),
        jnp.transpose(grad_qkv, (1, 0, 2)),
        grad_qv,
        grad_out,
        grad_branch,
        grad_gain,
        grad_shift,
        grad_up,
        grad_upb.reshape(-1),
        grad_down.T,
        grad_pool,
        grad_poolb.reshape(-1),
        grad_class.T,
        grad_classb.reshape(-1),
    )


def solution(mesh):
    in_specs = (
        P("dp", None),
        P("dp", None),
        P("dp", None),
        P("dp", None),
        P(None, None, "tensor"),
        P(None, "tensor"),
        P("tensor", None),
        P(),
        P(),
        P(),
        P(None, "tensor"),
        P("tensor"),
        P("tensor", None),
        P(),
        P(),
        P(),
        P(),
    )
    out_specs = (
        P("dp", None),
        P("dp", None),
        P(),
        P(),
        P("dp", None, "tensor"),
        P(None, ("tensor", "dp")),
        P("tensor", "dp"),
        P(None, "dp"),
        P(None, "dp"),
        P(None, "dp"),
        P("dp", "tensor"),
        P(("tensor", "dp")),
        P("tensor", "dp"),
        P("dp", None),
        P("dp"),
        P("dp", None),
        P(),
    )
    return jax.shard_map(
        partial(on_device, mesh.shape["dp"]),
        mesh=mesh,
        in_specs=in_specs,
        out_specs=out_specs,
        check_vma=False,
    )
```

time: 698 us -> 186 us (0.27)
  waiting for transfers between devices: 509 us -> 0 us
  Pallas kernels: 0 us -> 181 us
  matrix products: 45 us -> 0 us
  other arithmetic: 43.9 us -> 0 us
  blocking collectives: 41.5 us -> 0 us
  local copies, waits for them, and re-layouts: 35.8 us -> 2.53 us
  between operations: 20.8 us -> 0.82 us
    reduce_scatter x4 -> x0, waiting for transfers between devices: 259 us -> none  [the longest x1 64.8 us: on_device(): lax.psum_scatter(grad_pool.astype(jnp.bfloat16), 'dp', scatter_dimension=...]
    pallas_call x0 -> x2, Pallas kernels: none -> 181 us  [the longest x1 104 us: on_device(): pl.pallas_call(partial(layer_kernel, n_dp), out_shape=[shape((token_count...]
    psum x4 -> x0, waiting for transfers between devices: 125 us -> none  [the longest x1 34.6 us: on_device(): lax.psum(times_transposed(d_qkv, flat_qkv).astype(jnp.bfloat16), 'tensor')]
    unnamed x14 -> x0, waiting for transfers between devices: 125 us -> none
    dot_general x24 -> x0, matrix products: 45 us -> none  [the longest x5 13.5 us: contract_rows(): lax.dot_general(first_mat, second_mat, (((0,), (0,)), ((), ())), preferre...]
    psum x1 -> x0, blocking collectives: 22 us -> none  [on_device(): totals, class_sums = lax.psum((local_totals, class_totals), 'dp')]
    unnamed x1 -> x0, blocking collectives: 19.5 us -> none
    unnamed x133 -> x0, local copies, waits for them, and re-layouts: 18.4 us -> none
  transfers between devices with their start and end apart: 11 -> 0, of which waited for: 11 -> 0; matrix products, arithmetic and copies ran while one was open for 9% -> 0% of each run, Pallas kernels for 0% -> 0%
where the time goes in v1:
time: 186 us; the launch traced here: 184 us
  Pallas kernels  181 us (97%)
  local copies, waits for them, and re-layouts  2.53 us (1%)
    pallas_call x1, Pallas kernels, on_device(): pl.pallas_call(partial(layer_kernel, n_dp), out_shape=[shape((token_count...  104 us
    pallas_call x1, Pallas kernels, on_device(): pl.pallas_call(partial(place_kernel, n_dp), out_shape=[shape((token_count...  77.3 us

profile of v1, /device:TPU:0, one launch (start us, length us, event | category | flops | bytes accessed | tf_op | source)
XLA Modules:
  0.0 184.4 jit_solution(15525952736718032107)
XLA Ops:
  0.7 1.3 reshape.62.upb_ref
  1.9 1.3 reshape.63.pb_ref
  3.2 103.7 %layer.1 = (bf16[512,768]{1,0:T(8,128)(2,1)}, bf16[512,768]{1,0:T(8,128)(2,1)}, f32[96,768]{1,0:T(8,128)}, f32[96,768]{1,0:T(8,128)}, f32[96,768]{1,0:T(8,128)}, /*index=5*/f32[96,768]{1,0:T(8,128)}, f32[16,768]{1,0:T(8,128)}) custom-call(bf16[512,768]{1,0:T(8,128)(2,1)} %tok_hbm.1, bf16[512,768]{1,0:T(8,128)(2,1)} %cot_hbm.1, s32[1,16]{1,0:T(1,128)} %len_ref.1, ...), custom_call_target="tpu_custom_call" | custom-call | tf_op jit(solution)/shard_map/layer/pallas_call | solution.py:850
  106.9 77.3 %place.1 = (bf16[512,768]{1,0:T(8,128)(2,1)}, bf16[512,768]{1,0:T(8,128)(2,1)}, f32[1,1]{1,0:T(1,128)}, f32[1,1]{1,0:T(1,128)}, f32[3,96,192]{2,1,0:T(8,128)}, /...) custom-call(bf16[512,768]{1,0:T(8,128)(2,1)} %get-tuple-element.41.b, ...), custom_call_target="tpu_custom_call" | custom-call | tf_op jit(solution)/shard_map/place/pallas_call | solution.py:906

commit v2 on v1

v2 whole, which is shorter than its diff:
```python
from functools import partial

import jax
import jax.numpy as jnp
from jax import lax
from jax.experimental import pallas as pl
from jax.experimental.pallas import tpu as pltpu
from jax.sharding import PartitionSpec as P

HD = 64
MESH = pl.DeviceIdType.MESH
F32 = jnp.float32
BF16 = jnp.bfloat16
masked_score = -1e30
norm_eps = 1e-12
SQRT_HALF = 0.7071067811865476
PDF_SCALE = 0.3989422804014327
VEC_ROWS = 16
PLAN = (
    "I_y", "fdS", "fdO", "fuS", "fuO", "ln1b0", "FD_11", "FD_10", "I_r", "FU_11",
    "FU_10", "ln1b1", "dctx", "ab0", "ab1", "FD_01", "ab2", "FU_01", "ab3", "ab4",
    "SD_1", "ab5", "dattT", "FD_00", "SU_1", "dsum", "fqS", "SD_0", "dtok0", "I_q",
    "dtok1", "SU_0", "fqO", "qv", "V_y", "FU_00", "LD", "gtok0", "I_c", "FQ_11",
    "pool", "LU", "V_r", "gtok1", "FQ_10", "FQ_01", "ED", "SQ_1", "FQ_00", "SQ_0",
    "V_q", "EU", "LQ", "V_e", "EQ",
)
VMEM_LIMIT = 56 * 1024 * 1024


def dot_nn(a, b):
    return lax.dot_general(a, b, (((1,), (0,)), ((), ())), preferred_element_type=F32)


def dot_nt(a, b):
    return lax.dot_general(a, b, (((1,), (1,)), ((), ())), preferred_element_type=F32)


def dot_tn(a, b):
    return lax.dot_general(a, b, (((0,), (0,)), ((), ())), preferred_element_type=F32)


def row_mean(v):
    return jnp.sum(v, axis=1, keepdims=True) * (1.0 / v.shape[1])


def col_sum(v):
    return jnp.sum(v, axis=0, keepdims=True)


def norm_forward(values):
    centered = values - row_mean(values)
    inv_scale = lax.rsqrt(row_mean(centered * centered) + norm_eps)
    return centered * inv_scale, inv_scale


def norm_backward(gradient, normed, inv_scale, gain_row):
    scaled = gradient * gain_row
    inner = scaled - row_mean(scaled) - normed * row_mean(scaled * normed)
    return inner * inv_scale


def gelu_parts(pre_act):
    cdf = 0.5 * (1.0 + lax.erf(pre_act * SQRT_HALF))
    pdf = PDF_SCALE * jnp.exp(-0.5 * pre_act * pre_act)
    return pre_act * cdf, cdf + pre_act * pdf


class Stop(Exception):
    pass


STOP = None


def mark(name):
    if STOP is not None and name == STOP:
        raise Stop()


class Tracked:
    def __init__(self, copy):
        self.copy, self.received = copy, False

    def wait_recv(self):
        if not self.received:
            self.received = True
            self.copy.wait_recv()

    def wait_send(self):
        self.copy.wait_send()


class Copies:
    def __init__(self, send_sems, recv_sems):
        self.send_sems, self.recv_sems, self.used, self.open = send_sems, recv_sems, 0, []

    def start(self, src, dst, device):
        copy = pltpu.make_async_remote_copy(
            src_ref=src,
            dst_ref=dst,
            send_sem=self.send_sems.at[self.used],
            recv_sem=self.recv_sems.at[self.used],
            device_id=device,
            device_id_type=MESH,
        )
        self.used += 1
        copy.start()
        copy = Tracked(copy)
        self.open.append(copy)
        return copy

    def finish(self):
        for copy in self.open:
            copy.wait_send()


class Loads:
    def __init__(self, sems):
        self.sems, self.used = sems, 0

    def start(self, src, dst):
        copy = pltpu.make_async_copy(src, dst, self.sems.at[self.used])
        self.used += 1
        copy.start()
        return copy


def remote_copy_count(pairs):
    return 40 + 3 * (2 + 4 * pairs) + 4 * pairs


def layer_kernel(
    n_dp,
    tok_hbm,
    cot_hbm,
    len_ref,
    lab_ref,
    wqkv_hbm,
    qvb_ref,
    wout_hbm,
    bb_ref,
    ng_ref,
    ns_ref,
    wup_hbm,
    upb_ref,
    wdn_hbm,
    wpool_hbm,
    pb_ref,
    wcls_ref,
    cb_ref,
    bout_out,
    gtok_out,
    gqkvo_out,
    gup_out,
    gdn_out,
    gpool_out,
    vec_out,
    tok,
    cot,
    wt,
    wo,
    wup,
    wdn,
    wpool,
    up_bias,
    bias_mask,
    k_pad,
    v_pad,
    k_tr,
    v_tr,
    q_pad,
    q_away,
    probs,
    ctx,
    hid,
    hid_low,
    hid_tr,
    tok_tr,
    n_one,
    scale_one,
    act_low,
    d_gelu,
    acc,
    parts,
    d_sec,
    d_br,
    d_br_tr,
    d_pre_low,
    d_first,
    d_att,
    d_att_tr,
    d_ctx,
    d_kv_f32,
    d_kv_send,
    d_kv_recv,
    d_qkv,
    g_send,
    g_recv,
    g_own,
    first_send,
    first_recv,
    second_send,
    second_recv,
    last_send,
    last_recv,
    pool_fin,
    items,
    items_c,
    item_all,
    vec,
    vec_c,
    vec_s,
    vec_y,
    vec_t,
    vec_r,
    vec_q,
    cnt,
    cnt_y,
    cnt_s,
    cnt_r,
    cnt_q,
    load_sems,
    send_sems,
    recv_sems,
):
    pairs = n_dp // 4
    dp = lax.axis_index("dp")
    me = lax.axis_index("tensor")
    x = me // 2
    c = lax.rem(me, 2)
    y = lax.rem(dp, 2)
    r = lax.rem(dp // 2, 2)
    q = dp // 4
    core_dev = (dp, me + 1 - 2 * c)
    x_dev = (dp, 2 * (1 - x) + c)
    y_dev = (dp + 1 - 2 * y, me)
    r_dev = (dp + 2 - 4 * r, me)

    def q_of(k):
        return lax.rem(q + k, pairs)

    def q_dev(k):
        return (q_of(k) * 4 + r * 2 + y, me)

    away = range(1, pairs)
    token_count, width = tok.shape
    half = token_count // 2
    local_width = wo.shape[1]
    heads = local_width // HD
    slots = len_ref.shape[1]
    shard = width // n_dp
    chunk = 128
    chunks = half // chunk
    tile = 256
    tiles = width // tile
    own_rows = pl.ds(pl.multiple_of(c * half, half), half)
    away_rows = pl.ds(pl.multiple_of((1 - c) * half, half), half)

    barrier = pltpu.get_barrier_semaphore()
    peers = [core_dev, x_dev, y_dev, r_dev] + [q_dev(k) for k in away]
    for peer in peers:
        pl.semaphore_signal(barrier, inc=1, device_id=peer, device_id_type=MESH)

    loads = Loads(load_sems)
    remote = Copies(send_sems, recv_sems)
    load_tok = loads.start(tok_hbm, tok)
    load_wt = loads.start(wqkv_hbm, wt.at[c])
    load_wo = loads.start(wout_hbm, wo.at[c])
    load_wup = loads.start(wup_hbm, wup.at[c])
    load_wdn = loads.start(wdn_hbm, wdn.at[c])
    load_pool = loads.start(wpool_hbm, wpool)
    load_cot = loads.start(cot_hbm.at[own_rows], cot)

    lengths = [len_ref[0, i] for i in range(slots)]
    ends, total = [], 0
    for i in range(slots):
        total = total + lengths[i]
        ends.append(total)
    firsts = [jnp.minimum(ends[i] - lengths[i], token_count - 1) for i in range(slots)]
    key_place = lax.broadcasted_iota(jnp.int32, (token_count, 128), 0)
    query_place = lax.broadcasted_iota(jnp.int32, (8, half), 1) + c * half
    key_segment = jnp.zeros((token_count, 128), jnp.int32)
    query_segment = jnp.zeros((8, half), jnp.int32)
    for i in range(slots):
        key_segment = key_segment + (key_place >= ends[i]).astype(jnp.int32)
        query_segment = query_segment + (query_place >= ends[i]).astype(jnp.int32)
    for n in range(half // 128):
        cols = slice(n * 128, (n + 1) * 128)
        bias_mask[:, cols] = jnp.where(key_segment == query_segment[0:1, cols], 0.0, masked_score)
    item_row = lax.broadcasted_iota(jnp.int32, (slots, 128), 0)
    first_col = jnp.zeros((slots, 128), jnp.int32)
    len_col = jnp.zeros((slots, 128), jnp.int32)
    lab_col = jnp.zeros((slots, 128), jnp.int32)
    for i in range(slots):
        first_col = first_col + jnp.where(item_row == i, firsts[i], 0)
        len_col = len_col + jnp.where(item_row == i, lengths[i], 0)
        lab_col = lab_col + jnp.where(item_row == i, lab_ref[0, i], 0)
    live_all = jnp.where(len_col > 0, 1.0, 0.0)
    cnt[...] = jnp.broadcast_to(col_sum(live_all), cnt.shape)
    lane_item = lax.broadcasted_iota(jnp.int32, (1, 2 * slots), 1)
    first_row = jnp.zeros((1, 2 * slots), jnp.int32)
    for i in range(slots):
        first_row = first_row + jnp.where((lane_item == i) | (lane_item == i + slots), firsts[i], 0)

    up_bias[c] = jnp.broadcast_to(upb_ref[...].astype(F32).reshape(1, width), (8, width))
    vec[...] = jnp.zeros_like(vec)
    pad_rows = q_pad.shape[1] - local_width
    for b in range(2):
        q_pad[b, local_width:, :] = jnp.zeros((pad_rows, half), BF16)
        d_ctx[b, local_width:, :] = jnp.zeros((pad_rows, half), BF16)
        v_pad[b, :, local_width:] = jnp.zeros((token_count, pad_rows), BF16)

    def bias_cols(part, columns):
        row = qvb_ref[part : part + 1, :]
        block = jnp.transpose(jnp.broadcast_to(row, (128, local_width)))
        return jnp.concatenate([block] * (columns // 128), axis=1)

    load_tok.wait()
    load_wt.wait()
    rows_q, rows_k, rows_v = [slice(p * local_width, (p + 1) * local_width) for p in range(3)]
    query_bias = bias_cols(0, half)
    q_away[...] = (dot_nt(wt[c, rows_q, :], tok[away_rows, :]) + query_bias).astype(BF16)
    wide_k = jnp.concatenate([wt[c, rows_k, :], jnp.zeros((pad_rows, width), BF16)], axis=0)
    k_pad[c] = dot_nt(tok[...], wide_k).astype(BF16)
    v_tr[c] = (dot_nt(wt[c, rows_v, :], tok[...]) + bias_cols(1, token_count)).astype(BF16)
    q_pad[c, 0:local_width, :] = (dot_nt(wt[c, rows_q, :], tok[own_rows, :]) + query_bias).astype(BF16)

    pl.semaphore_wait(barrier, len(peers))
    mark("sends")
    send_q = remote.start(q_away, q_pad.at[c, pl.ds(0, local_width)], core_dev)
    send_k = remote.start(k_pad.at[c], k_pad.at[c], core_dev)
    send_v = remote.start(v_tr.at[c], v_tr.at[c], core_dev)
    send_wo = remote.start(wout_hbm, wo.at[c], core_dev)
    send_bias = remote.start(up_bias.at[c], up_bias.at[c], core_dev)
    send_wup = remote.start(wup_hbm, wup.at[c], core_dev)
    send_wdn = remote.start(wdn_hbm, wdn.at[c], core_dev)
    send_cnt_y = remote.start(cnt, cnt_y, y_dev)
    send_wt = remote.start(wqkv_hbm, wt.at[c], core_dev)

    half_row = lax.broadcasted_iota(jnp.int32, (128, half), 0) < HD
    inv_root = HD ** (-0.5)

    def half_of(block, i):
        if i == heads - 1 and i % 2 == 0:
            return block
        zero = jnp.zeros_like(block)
        return jnp.where(half_row, block, zero) if i % 2 == 0 else jnp.where(half_row, zero, block)

    def pair_of(i):
        return slice((i // 2) * 128, (i // 2 + 1) * 128)

    def attend(core):
        for i in range(heads):
            head_rows = slice(i * HD, (i + 1) * HD)
            scores = dot_nn(k_pad[core, :, pair_of(i)], half_of(q_pad[core, pair_of(i), :], i))
            scores = scores * inv_root + bias_mask[...]
            terms = jnp.exp(scores - jnp.max(scores, axis=0, keepdims=True))
            weights = terms * (1.0 / col_sum(terms))
            probs[core, i] = weights
            ctx[core, head_rows, :] = dot_nn(v_tr[core, head_rows, :], weights.astype(BF16)).astype(BF16)

    mark("attn_own")
    attend(c)
    send_q.wait_recv()
    send_k.wait_recv()
    send_v.wait_recv()
    mark("attn_other")
    attend(1 - c)
    mark("out")
    load_wo.wait()
    send_wo.wait_recv()

    def chunk_of(i):
        return slice(i * chunk, (i + 1) * chunk)

    def exchange(which, i):
        block = parts.at[which, x, chunk_of(i)]
        return remote.start(block, block, x_dev)

    def both_parts(which, i):
        return parts[which, 0, chunk_of(i), :].astype(F32) + parts[which, 1, chunk_of(i), :].astype(F32)

    ATT, FFN, HIDDEN, TOKEN = 0, 1, 2, 3
    send_att = []
    for i in range(chunks):
        rows = chunk_of(i)
        partial_sum = dot_tn(ctx[0, :, rows], wo[0]) + dot_tn(ctx[1, :, rows], wo[1])
        parts[ATT, x, rows, :] = partial_sum.astype(BF16)
        send_att.append(exchange(ATT, i))
    send_cnt_y.wait_recv()
    cnt_s[...] = cnt[...] + cnt_y[...]
    send_cnt_r = remote.start(cnt_s, cnt_r, r_dev)

    mark("transposes")
    for b in range(2):
        k_tr[b] = jnp.transpose(k_pad[b])[0:local_width, :]
        v_pad[b, :, 0:local_width] = jnp.transpose(v_tr[b])
    tok_tr[...] = jnp.transpose(tok[own_rows, :])

    mark("ffn_f")
    load_wup.wait()
    load_wdn.wait()
    send_ffn = []
    for i in range(chunks):
        rows = chunk_of(i)
        send_att[i].wait_recv()
        token_rows = pl.ds(pl.multiple_of(c * half + i * chunk, chunk), chunk)
        attention = both_parts(ATT, i) + bb_ref[0:1, :]
        normed, inv_scale = norm_forward(tok[token_rows, :].astype(F32) + attention)
        n_one[rows, :] = normed
        scale_one[rows, :] = inv_scale
        value = normed * ng_ref[0:1, :] + ns_ref[0:1, :]
        hid[rows, :] = value
        hid_low[rows, :] = value.astype(BF16)
        for b in range(2):
            core = c if b == 0 else 1 - c
            if i == 0 and b == 1:
                send_bias.wait_recv()
                send_wup.wait_recv()
            for n in range(tiles):
                cols = slice(n * tile, (n + 1) * tile)
                pre_act = dot_nn(hid_low[rows, :], wup[core, :, cols]) + up_bias[core, 0:1, cols]
                value, slope = gelu_parts(pre_act)
                act_low[b, rows, cols] = value.astype(BF16)
                d_gelu[b, rows, cols] = slope
            if i == 0 and b == 1:
                send_wdn.wait_recv()
            product = dot_nn(act_low[b, rows, :], wdn[core])
            if b == 0:
                acc[...] = product
            else:
                parts[FFN, x, rows, :] = (acc[...] + product).astype(BF16)
        send_ffn.append(exchange(FFN, i))
        if i == 0:
            send_cnt_r.wait_recv()
            cnt_q[q] = cnt_s[...] + cnt_r[...]
            send_cnt_q = [remote.start(cnt_q.at[q], cnt_q.at[q], q_dev(k)) for k in away]

    mark("hid_tr")
    hid_tr[...] = jnp.transpose(hid_low[...])
    load_pool.wait()
    load_cot.wait()
    for copy in send_cnt_q:
        copy.wait_recv()
    item_count = cnt_q[0]
    for k in away:
        item_count = item_count + cnt_q[k]
    inv_count = 1.0 / item_count[0:1, 0:1]

    classes = wcls_ref.shape[0]
    class_rows = wcls_ref[...].astype(F32)
    class_pad = jnp.concatenate([class_rows, jnp.zeros((16 - classes, width), F32)], axis=0).astype(BF16)
    class_lane = lax.broadcasted_iota(jnp.int32, (slots, 16), 1)
    class_bias = jnp.zeros((slots, 16), F32)
    for k in range(classes):
        class_bias = class_bias + jnp.where(class_lane == k, cb_ref[0, k], 0.0)
    label_hot = jnp.where(class_lane == lab_col[:, 0:1], 1.0, 0.0)
    lane = lax.broadcasted_iota(jnp.int32, (1, 128), 1)

    def add_rows(first, value):
        vec[first : first + value.shape[0], 0 : value.shape[1]] += value

    mark("ln2")
    up_sums = [[None] * tiles, [None] * tiles]
    send_hidden = []
    for i in range(chunks):
        rows = chunk_of(i)
        place = c * half + i * chunk
        send_ffn[i].wait_recv()
        normed, inv_scale = norm_forward(hid[rows, :] + (both_parts(FFN, i) + bb_ref[1:2, :]))
        low = (normed * ng_ref[1:2, :] + ns_ref[1:2, :]).astype(BF16)
        bout_out[pl.ds(pl.multiple_of(place, chunk), chunk), :] = low

        local_first = first_col[:, 0:1] - place
        pick = (lax.broadcasted_iota(jnp.int32, (slots, chunk), 1) == local_first).astype(F32).astype(BF16)
        picked = dot_nn(pick, low).astype(BF16)
        pooled = jnp.tanh(dot_nn(picked, wpool[...]) + pb_ref[...].reshape(1, width))
        pooled_low = pooled.astype(BF16)
        logits = jnp.where(class_lane < classes, dot_nt(pooled_low, class_pad) + class_bias, masked_score)
        shifted = logits - jnp.max(logits, axis=1, keepdims=True)
        log_probs = shifted - jnp.log(jnp.sum(jnp.exp(shifted), axis=1, keepdims=True))
        class_probs = jnp.exp(log_probs)
        owned = jnp.where((local_first >= 0) & (local_first < chunk), live_all[:, 0:1], 0.0)
        item_ce = -jnp.sum(label_hot * log_probs, axis=1, keepdims=True) * owned
        item_ent = -jnp.sum(class_probs * log_probs, axis=1, keepdims=True) * owned
        d_logits = (class_probs - label_hot) * (owned * inv_count)
        d_pooled = jnp.zeros((slots, width), F32)
        for k in range(classes):
            d_pooled = d_pooled + d_logits[:, k : k + 1] * class_rows[k : k + 1, :]
            add_rows(7 + k, col_sum(d_logits[:, k : k + 1] * pooled_low.astype(F32)))
        d_pre = (d_pooled * (1.0 - pooled * pooled)).astype(BF16)
        add_rows(6, col_sum(d_pre.astype(F32)))
        add_rows(
            10, jnp.where(lane == 0, col_sum(item_ce), 0.0) + jnp.where(lane == 1, col_sum(item_ent), 0.0)
        )
        vec[10:11, 128:144] += col_sum(d_logits)
        if i == 0:
            items[0] = picked
            items[1] = d_pre
        else:
            items[0] += picked
            items[1] += d_pre
        if i == chunks - 1:
            send_items = remote.start(items.at[1 - c], items_c, core_dev)
        d_picked = dot_nt(d_pre, wpool[...])
        d_high = d_picked.astype(BF16)
        d_both = jnp.concatenate([d_high, (d_picked - d_high.astype(F32)).astype(BF16)], axis=0)

        token_place = lax.broadcasted_iota(jnp.int32, (chunk, 2 * slots), 0) + place
        spread = dot_nn((token_place == first_row).astype(F32).astype(BF16), d_both)
        live = jnp.where(token_place[:, 0:1] < total, 1.0, 0.0)
        d_output = cot[rows, :].astype(F32) * live + spread
        add_rows(3, col_sum(d_output * normed))
        add_rows(5, col_sum(d_output))
        d_second = norm_backward(d_output, normed, inv_scale, ng_ref[1:2, :])
        add_rows(1, col_sum(d_second))
        d_sec[rows, :] = d_second
        d_br[rows, :] = d_second.astype(BF16)
        for b in range(2):
            core = c if b == 0 else 1 - c
            for n in range(tiles):
                cols = slice(n * tile, (n + 1) * tile)
                d_act = dot_nt(d_br[rows, :], wdn[core, cols, :])
                low = (d_act * d_gelu[b, rows, cols]).astype(BF16)
                d_pre_low[b, rows, cols] = low
                up_sum = col_sum(low.astype(F32))
                up_sums[b][n] = up_sum if i == 0 else up_sums[b][n] + up_sum
            product = dot_nt(d_pre_low[b, rows, :], wup[core])
            if b == 0:
                acc[...] = product
            else:
                parts[HIDDEN, x, rows, :] = (acc[...] + product).astype(BF16)
        send_hidden.append(exchange(HIDDEN, i))
    vec[pl.ds(11 + c, 1), :] = jnp.concatenate(up_sums[0], axis=1)
    vec[pl.ds(12 - c, 1), :] = jnp.concatenate(up_sums[1], axis=1)
    send_out = remote.start(bout_out.at[own_rows], bout_out.at[own_rows], core_dev)

    DOWN, UP, QKVO = 0, 1, 2
    along = {DOWN: (r, y, r_dev, y_dev), UP: (y, r, y_dev, r_dev), QKVO: (y, r, y_dev, r_dev)}
    row_major = {DOWN: True, UP: False, QKVO: False}
    reach = {1: list(away), 0: [0]}
    slot_of = {(flip, k): (1 - flip) * pairs + (k - 1) % pairs for flip in range(2) for k in range(pairs)}
    sent = {}
    step = {}

    def store_blocks(out, block, cols, product):
        for j in range(n_dp):
            value = product[j * shard : (j + 1) * shard, :].astype(out.dtype)
            bits = (j % 2, (j // 2) % 2)
            if row_major[block]:
                bits = bits[::-1]
            out[block, bits[0], bits[1], j // 4, :, cols] = value

    def fill(out, block, product_of):
        for n in range(tiles):
            cols = slice(n * tile, (n + 1) * tile)
            store_blocks(out, block, cols, product_of(cols))

    def core_send(block):
        first = along[block][0]
        for name, side in (("away", 1 - first), ("kept", first)):
            sent[block, name] = remote.start(g_send.at[block, side], g_recv.at[block, side], core_dev)

    def after_core(block, name, first_value, second_value, q_index):
        sent[block, name].wait_recv()
        index = (block, first_value, second_value, q_index)
        return g_own[index] + g_recv[index].astype(F32)

    def first_step(block, flip, group):
        first, second, device, _ = along[block]
        for k in reach[group]:
            slot = slot_of[flip, k]
            value = after_core(block, "away", 1 - first, 1 - second if flip else second, q_of(k))
            first_send[block, slot] = value.astype(BF16)
            sent[block, 1, flip, k] = remote.start(first_send.at[block, slot], first_recv.at[block, slot], device)

    def first_sum(block, flip, k):
        first, second, _, _ = along[block]
        sent[block, 1, flip, k].wait_recv()
        value = after_core(block, "kept", first, 1 - second if flip else second, q_of(k))
        return value + first_recv[block, slot_of[flip, k]].astype(F32)

    def second_step(block, group):
        for k in reach[group]:
            second_send[block, k] = first_sum(block, 1, k).astype(BF16)
            sent[block, 2, k] = remote.start(second_send.at[block, k], second_recv.at[block, k], along[block][3])

    def second_sum(block, k):
        sent[block, 2, k].wait_recv()
        return first_sum(block, 0, k) + second_recv[block, k].astype(F32)

    def last_step(block):
        for k in away:
            last_send[block, k - 1] = second_sum(block, k).astype(BF16)
            sent[block, 3, k] = remote.start(last_send.at[block, k - 1], last_recv.at[block, k - 1], q_dev(k))

    def end_step(block, out):
        result = second_sum(block, 0)
        for k in away:
            sent[block, 3, k].wait_recv()
            result = result + last_recv[block, k - 1].astype(F32)
        out[...] = result

    for letter, block, out in (("D", DOWN, gdn_out), ("U", UP, gup_out), ("Q", QKVO, gqkvo_out)):
        for group in range(2):
            for flip in range(2):
                step["F%s_%d%d" % (letter, flip, group)] = partial(first_step, block, flip, group)
            step["S%s_%d" % (letter, group)] = partial(second_step, block, group)
        step["L" + letter] = partial(last_step, block)
        step["E" + letter] = partial(end_step, block, out)

    def fill_down_send():
        d_br_tr[...] = jnp.transpose(d_br[...])
        fill(g_send, DOWN, lambda cols: dot_nn(d_br_tr[...], act_low[1, :, cols]))
        core_send(DOWN)

    def fill_up_send():
        fill(g_send, UP, lambda cols: dot_nn(hid_tr[...], d_pre_low[1, :, cols]))
        core_send(UP)

    step["fdS"] = fill_down_send
    step["fdO"] = lambda: fill(g_own, DOWN, lambda cols: dot_nn(d_br_tr[...], act_low[0, :, cols]))
    step["fuS"] = fill_up_send
    step["fuO"] = lambda: fill(g_own, UP, lambda cols: dot_nn(hid_tr[...], d_pre_low[0, :, cols]))

    def item_rows(first, count):
        return pl.ds(pl.multiple_of(first * slots, count * slots), count * slots)

    def pass_items(name, rows, devices):
        sent[name] = [remote.start(item_all.at[c, rows], item_all.at[c, rows], device) for device in devices]

    def settle(name):
        for copy in sent[name]:
            copy.wait_recv()

    def items_y():
        send_items.wait_recv()
        item_all[c, item_rows(dp, 1), :] = items[c] + items_c[...]
        pass_items("items_y", item_rows(dp, 1), [y_dev])

    def items_r():
        settle("items_y")
        pass_items("items_r", item_rows(dp - y, 2), [r_dev])

    def items_q():
        settle("items_r")
        pass_items("items_q", item_rows(q * 4, 4), [q_dev(k) for k in away])

    def items_core():
        settle("items_q")
        sent["items_core"] = [remote.start(item_all.at[c], item_all.at[c], core_dev)]

    def pool():
        settle("items_core")
        pool_fin[...] = dot_tn(item_all[0], item_all[1])
        gpool_out[...] = pool_fin[pl.ds(pl.multiple_of(dp * shard, 8), shard), :]

    step.update(I_y=items_y, I_r=items_r, I_q=items_q, I_c=items_core, pool=pool)

    def norm_one_back(i):
        rows = chunk_of(i)
        send_hidden[i].wait_recv()
        d_hidden = both_parts(HIDDEN, i) + d_sec[rows, :]
        normed = n_one[rows, :]
        add_rows(2, col_sum(d_hidden * normed))
        add_rows(4, col_sum(d_hidden))
        gradient = norm_backward(d_hidden, normed, scale_one[rows, :], ng_ref[0:1, :])
        add_rows(0, col_sum(gradient))
        d_first[rows, :] = gradient
        d_att[rows, :] = gradient.astype(BF16)

    def context_back():
        for b in range(2):
            d_ctx[b, 0:local_width, :] = dot_nt(wo[b], d_att[...]).astype(BF16)

    def head_back(n):
        b, i = n // heads, n % heads
        head_rows = slice(i * HD, (i + 1) * HD)
        d_probs = dot_nn(v_pad[b, :, pair_of(i)], half_of(d_ctx[b, pair_of(i), :], i))
        weights = probs[b, i]
        delta = col_sum(weights * d_probs)
        d_scores = (weights * (d_probs - delta)).astype(BF16)
        d_value = dot_nt(d_ctx[b, head_rows, :], weights.astype(BF16))
        d_key = dot_nt(q_pad[b, head_rows, :], d_scores) * inv_root
        d_query = dot_nn(k_tr[b, head_rows, :], d_scores) * inv_root
        d_qkv[b, head_rows, :] = d_query.astype(BF16)
        for part, value in ((0, d_key), (1, d_value)):
            part_rows = slice(part * local_width + i * HD, part * local_width + (i + 1) * HD)
            for side in range(2):
                lanes = slice(side * half, (side + 1) * half)
                d_kv_f32[side, b, part_rows, :] = value[:, lanes]
                d_kv_send[side, b, part_rows, :] = value[:, lanes].astype(BF16)
        if n == 2 * heads - 1:
            sent["kv"] = remote.start(d_kv_send.at[1 - c], d_kv_recv, core_dev)

    def turn_attention():
        d_att_tr[...] = jnp.transpose(d_att[...])

    def join_cores():
        sent["kv"].wait_recv()
        for b in range(2):
            d_qkv[b, local_width:, :] = (d_kv_f32[c, b] + d_kv_recv[b].astype(F32)).astype(BF16)

    for i in range(chunks):
        step["ln1b%d" % i] = partial(norm_one_back, i)
    step["dctx"] = context_back
    for n in range(2 * heads):
        step["ab%d" % n] = partial(head_back, n)
    step["dattT"] = turn_attention
    step["dsum"] = join_cores

    def fill_qkvo(core, out):
        first_part = dot_nt(tok_tr[...], d_qkv[core])
        second_part = dot_nt(d_att_tr[...], ctx[core])
        store_blocks(out, QKVO, slice(0, width), jnp.concatenate([first_part, second_part], axis=1))

    def fill_qkvo_send():
        fill_qkvo(1 - c, g_send)
        core_send(QKVO)

    def token_part(i):
        send_wt.wait_recv()
        rows = chunk_of(i)
        partial_sum = dot_tn(d_qkv[0, :, rows], wt[0]) + dot_tn(d_qkv[1, :, rows], wt[1])
        parts[TOKEN, x, rows, :] = partial_sum.astype(BF16)
        sent["token", i] = exchange(TOKEN, i)

    def token_end(i):
        sent["token", i].wait_recv()
        rows = chunk_of(i)
        place = pl.ds(pl.multiple_of(c * half + i * chunk, chunk), chunk)
        gtok_out[place, :] = (both_parts(TOKEN, i) + d_first[rows, :]).astype(BF16)
        if i == chunks - 1:
            sent["gtok"] = remote.start(gtok_out.at[own_rows], gtok_out.at[own_rows], core_dev)

    step["fqS"] = fill_qkvo_send
    step["fqO"] = lambda: fill_qkvo(c, g_own)
    for i in range(chunks):
        step["dtok%d" % i] = partial(token_part, i)
        step["gtok%d" % i] = partial(token_end, i)

    def vec_core():
        ones = jnp.ones((8, half), BF16)
        sums = [dot_nt(ones, d_qkv[b])[0:1, :] for b in range(2)]
        columns = [v[:, :local_width] for v in sums] + [v[:, 2 * local_width :] for v in sums]
        vec[13:14, :] = jnp.concatenate(columns, axis=1)
        vec[14:15, 0:128] = item_count[0:1, :]
        sent["vec"] = remote.start(vec, vec_c, core_dev)

    def vec_along_y():
        sent["vec"].wait_recv()
        vec_s[...] = vec[...] + vec_c[...]
        sent["vec_y"] = remote.start(vec_s, vec_y, y_dev)

    def vec_along_r():
        sent["vec_y"].wait_recv()
        vec_t[...] = vec_s[...] + vec_y[...]
        sent["vec_r"] = remote.start(vec_t, vec_r, r_dev)

    def vec_along_q():
        sent["vec_r"].wait_recv()
        vec_q[q] = vec_t[...] + vec_r[...]
        sent["vec_q"] = [remote.start(vec_q.at[q], vec_q.at[q], q_dev(k)) for k in away]

    def vec_end():
        settle("vec_q")
        vec_total = vec_q[0]
        for k in away:
            vec_total = vec_total + vec_q[k]
        vec_out[...] = vec_total

    step.update(qv=vec_core, V_y=vec_along_y, V_r=vec_along_r, V_q=vec_along_q, V_e=vec_end)

    assert sorted(PLAN) == sorted(step)
    for name in PLAN:
        mark(name)
        step[name]()
    mark("finish")
    send_out.wait_recv()
    sent["gtok"].wait_recv()
    remote.finish()


def place_kernel(
    n_dp,
    bout_in,
    gtok_in,
    gqkvo_in,
    gup_in,
    gdn_in,
    gpool_in,
    vec_in,
    bout,
    gtok,
    loss,
    entropy,
    gqkv,
    gqv,
    gout,
    gbranch,
    ggain,
    gshift,
    gup,
    gupb,
    gdn,
    gpool,
    gpoolb,
    gclass,
    gclassb,
    sems,
):
    moves = ((bout_in, bout), (gtok_in, gtok), (gup_in, gup), (gdn_in, gdn), (gpool_in, gpool))
    copies = [pltpu.make_async_copy(src, dst, sems.at[i]) for i, (src, dst) in enumerate(moves)]
    for copy in copies:
        copy.start()
    dp = lax.axis_index("dp")
    c = lax.rem(lax.axis_index("tensor"), 2)
    width = vec_in.shape[1]
    shard = width // n_dp
    local_width = gout.shape[0]
    for part in range(3):
        gqkv[part] = gqkvo_in[:, part * local_width : (part + 1) * local_width]
    gout[...] = jnp.transpose(gqkvo_in[:, 3 * local_width :])
    sums = vec_in[...]
    mine = pltpu.roll(sums, lax.rem(width - dp * shard, width), axis=1)
    gbranch[...] = mine[0:2, :shard]
    ggain[...] = mine[2:4, :shard]
    gshift[...] = mine[4:6, :shard]
    gpoolb[...] = mine[6:7, :shard]
    gclass[...] = mine[7 : 7 + gclass.shape[0], :shard]
    gupb[...] = jnp.where(c == 0, mine[11:12, :shard], mine[12:13, :shard])
    small = local_width // n_dp
    quarter = pltpu.roll(sums, lax.rem(width - (c * local_width + dp * small), width), axis=1)
    gqv[0:1, :] = quarter[13:14, :small]
    gqv[1:2, :] = quarter[13:14, 2 * local_width : 2 * local_width + small]
    inv_count = 2.0 * n_dp / sums[14:15, 0:1]
    loss[...] = sums[10:11, 0:1] * inv_count
    entropy[...] = sums[10:11, 1:2] * inv_count
    gclassb[...] = sums[10:11, 128 : 128 + gclassb.shape[1]]
    for copy in copies:
        copy.wait()


def on_device(
    n_dp,
    tokens,
    cotangent,
    lengths,
    labels,
    w_qkv,
    qv_bias,
    w_out,
    branch_bias,
    norm_gain,
    norm_shift,
    w_up,
    up_bias,
    w_down,
    w_pool,
    pool_bias,
    w_class,
    class_bias,
):
    token_count, width = tokens.shape
    local_width = w_out.shape[0]
    hidden = w_up.shape[1]
    classes = w_class.shape[1]
    slots = lengths.shape[1]
    pairs = n_dp // 4
    shard = width // n_dp
    half = token_count // 2
    heads = local_width // HD
    padded = (local_width + 127) // 128 * 128
    assert hidden == width and 4 * local_width == width and lengths.shape[0] == 1
    shape = jax.ShapeDtypeStruct
    anywhere = pl.BlockSpec(memory_space=pl.ANY)
    vmem = pl.BlockSpec(memory_space=pltpu.VMEM)
    smem = pl.BlockSpec(memory_space=pltpu.SMEM)
    blocks = (3, 2, 2, pairs, shard, width)
    copies = remote_copy_count(pairs)
    V = pltpu.VMEM
    scratch = dict(
        tok=V((token_count, width), BF16),
        cot=V((half, width), BF16),
        wt=V((2, 3 * local_width, width), BF16),
        wo=V((2, local_width, width), BF16),
        wup=V((2, width, hidden), BF16),
        wdn=V((2, hidden, width), BF16),
        wpool=V((width, width), BF16),
        up_bias=V((2, 8, width), F32),
        bias_mask=V((token_count, half), F32),
        k_pad=V((2, token_count, padded), BF16),
        v_pad=V((2, token_count, padded), BF16),
        k_tr=V((2, local_width, token_count), BF16),
        v_tr=V((2, local_width, token_count), BF16),
        q_pad=V((2, padded, half), BF16),
        q_away=V((local_width, half), BF16),
        probs=V((2, heads, token_count, half), F32),
        ctx=V((2, local_width, half), BF16),
        hid=V((half, width), F32),
        hid_low=V((half, width), BF16),
        hid_tr=V((width, half), BF16),
        tok_tr=V((width, half), BF16),
        n_one=V((half, width), F32),
        scale_one=V((half, 1), F32),
        act_low=V((2, half, hidden), BF16),
        d_gelu=V((2, half, hidden), F32),
        acc=V((128, width), F32),
        parts=V((4, 2, half, width), BF16),
        d_sec=V((half, width), F32),
        d_br=V((half, width), BF16),
        d_br_tr=V((width, half), BF16),
        d_pre_low=V((2, half, hidden), BF16),
        d_first=V((half, width), F32),
        d_att=V((half, width), BF16),
        d_att_tr=V((width, half), BF16),
        d_ctx=V((2, padded, half), BF16),
        d_kv_f32=V((2, 2, 2 * local_width, half), F32),
        d_kv_send=V((2, 2, 2 * local_width, half), BF16),
        d_kv_recv=V((2, 2 * local_width, half), BF16),
        d_qkv=V((2, 3 * local_width, half), BF16),
        g_send=V(blocks, BF16),
        g_recv=V(blocks, BF16),
        g_own=V(blocks, F32),
        first_send=V((3, 2 * pairs, shard, width), BF16),
        first_recv=V((3, 2 * pairs, shard, width), BF16),
        second_send=V((3, pairs, shard, width), BF16),
        second_recv=V((3, pairs, shard, width), BF16),
        last_send=V((3, pairs - 1, shard, width), BF16),
        last_recv=V((3, pairs - 1, shard, width), BF16),
        pool_fin=V((width, width), F32),
        items=V((2, slots, width), BF16),
        items_c=V((slots, width), BF16),
        item_all=V((2, n_dp * slots, width), BF16),
        vec=V((VEC_ROWS, width), F32),
        vec_c=V((VEC_ROWS, width), F32),
        vec_s=V((VEC_ROWS, width), F32),
        vec_y=V((VEC_ROWS, width), F32),
        vec_t=V((VEC_ROWS, width), F32),
        vec_r=V((VEC_ROWS, width), F32),
        vec_q=V((pairs, VEC_ROWS, width), F32),
        cnt=V((8, 128), F32),
        cnt_y=V((8, 128), F32),
        cnt_s=V((8, 128), F32),
        cnt_r=V((8, 128), F32),
        cnt_q=V((pairs, 8, 128), F32),
    )
    found = pl.pallas_call(
        partial(layer_kernel, n_dp),
        out_shape=[
            V((token_count, width), BF16),
            V((token_count, width), BF16),
            V((shard, width), F32),
            V((shard, width), F32),
            V((shard, width), F32),
            V((shard, width), F32),
            V((VEC_ROWS, width), F32),
        ],
        in_specs=[
            anywhere,
            anywhere,
            smem,
            smem,
            anywhere,
            vmem,
            anywhere,
            vmem,
            vmem,
            vmem,
            anywhere,
            vmem,
            anywhere,
            anywhere,
            vmem,
            vmem,
            smem,
        ],
        out_specs=[vmem] * 7,
        scratch_shapes=list(scratch.values())
        + [
            pltpu.SemaphoreType.DMA((8,)),
            pltpu.SemaphoreType.DMA((copies,)),
            pltpu.SemaphoreType.DMA((copies,)),
        ],
        compiler_params=pltpu.CompilerParams(
            collective_id=0, has_side_effects=True, vmem_limit_bytes=VMEM_LIMIT
        ),
        name="layer",
    )(
        tokens,
        cotangent,
        lengths,
        labels,
        jnp.transpose(w_qkv, (1, 2, 0)).reshape(3 * local_width, width),
        qv_bias,
        w_out,
        branch_bias,
        norm_gain,
        norm_shift,
        w_up,
        up_bias,
        w_down,
        w_pool,
        pool_bias,
        w_class.T,
        class_bias.reshape(1, classes),
    )
    small = local_width // n_dp
    placed = pl.pallas_call(
        partial(place_kernel, n_dp),
        out_shape=[
            shape((token_count, width), BF16),
            shape((token_count, width), BF16),
            shape((1, 1), F32),
            shape((1, 1), F32),
            shape((3, shard, local_width), F32),
            shape((2, small), F32),
            shape((local_width, shard), F32),
            shape((2, shard), F32),
            shape((2, shard), F32),
            shape((2, shard), F32),
            shape((shard, hidden), F32),
            shape((1, hidden // n_dp), F32),
            shape((shard, hidden), F32),
            shape((shard, width), F32),
            shape((1, shard), F32),
            shape((classes, shard), F32),
            shape((1, classes), F32),
        ],
        in_specs=[vmem] * 7,
        out_specs=[anywhere] * 2 + [vmem] * 8 + [anywhere, vmem, anywhere, anywhere] + [vmem] * 3,
        scratch_shapes=[pltpu.SemaphoreType.DMA((5,))],
        name="place",
    )(*[pltpu.with_memory_space_constraint(value, pltpu.VMEM) for value in found])
    (
        block_out,
        grad_tokens,
        loss,
        entropy,
        grad_qkv,
        grad_qv,
        grad_out,
        grad_branch,
        grad_gain,
        grad_shift,
        grad_up,
        grad_upb,
        grad_down,
        grad_pool,
        grad_poolb,
        grad_class,
        grad_classb,
    ) = placed
    return (
        block_out,
        grad_tokens,
        loss.reshape(()),
        entropy.reshape(()),
        jnp.transpose(grad_qkv, (1, 0, 2)),
        grad_qv,
        grad_out,
        grad_branch,
        grad_gain,
        grad_shift,
        grad_up,
        grad_upb.reshape(-1),
        grad_down.T,
        grad_pool,
        grad_poolb.reshape(-1),
        grad_class.T,
        grad_classb.reshape(-1),
    )


def solution(mesh):
    in_specs = (
        P("dp", None),
        P("dp", None),
        P("dp", None),
        P("dp", None),
        P(None, None, "tensor"),
        P(None, "tensor"),
        P("tensor", None),
        P(),
        P(),
        P(),
        P(None, "tensor"),
        P("tensor"),
        P("tensor", None),
        P(),
        P(),
        P(),
        P(),
    )
    out_specs = (
        P("dp", None),
        P("dp", None),
        P(),
        P(),
        P("dp", None, "tensor"),
        P(None, ("tensor", "dp")),
        P("tensor", "dp"),
        P(None, "dp"),
        P(None, "dp"),
        P(None, "dp"),
        P("dp", "tensor"),
        P(("tensor", "dp")),
        P("tensor", "dp"),
        P("dp", None),
        P("dp"),
        P("dp", None),
        P(),
    )
    return jax.shard_map(
        partial(on_device, mesh.shape["dp"]),
        mesh=mesh,
        in_specs=in_specs,
        out_specs=out_specs,
        check_vma=False,
    )
```

time: 186 us -> 85.2 us (0.46)
  Pallas kernels: 181 us -> 84.1 us
  local copies, waits for them, and re-layouts: 2.53 us -> 0 us
    pallas_call x1, Pallas kernels: 77.3 us -> 2.34 us  [on_device(): pl.pallas_call(partial(place_kernel, n_dp), out_shape=[shape((token_count...]
    pallas_call x1, Pallas kernels: 104 us -> 81.8 us  [on_device(): pl.pallas_call(partial(layer_kernel, n_dp), out_shape=[V((token_count, wi...]
    reshape x2 -> x0, local copies, waits for them, and re-layouts: 2.53 us -> none  [the longest x1 1.27 us: on_device(): pool_bias.reshape(1, width)]
where the time goes in v2:
time: 85.2 us; the launch traced here: 85 us
  Pallas kernels  84.1 us (99%)
    pallas_call x1, Pallas kernels, on_device(): pl.pallas_call(partial(layer_kernel, n_dp), out_shape=[V((token_count, wi...  81.8 us
    pallas_call x1, Pallas kernels, on_device(): pl.pallas_call(partial(place_kernel, n_dp), out_shape=[shape((token_count...  2.34 us

profile of v2, /device:TPU:0, one launch (start us, length us, event | category | flops | bytes accessed | tf_op | source)
XLA Modules:
  0.0 85.0 jit_solution(10098029795605721985)
XLA Ops:
  0.7 81.8 %layer.1 = (bf16[512,768]{1,0:T(8,128)(2,1)S(1)}, bf16[512,768]{1,0:T(8,128)(2,1)S(1)}, f32[96,768]{1,0:T(8,128)S(1)}, f32[96,768]{1,0:T(8,128)S(1)}, f32[96,768...) custom-call(bf16[512,768]{1,0:T(8,128)(2,1)} %tok_hbm.1, bf16[512,768]{1,0:T(8,128)(2,1)} %cot_hbm.1, ...), custom_call_target="tpu_custom_call" | custom-call | tf_op jit(solution)/shard_map/layer/pallas_call | solution.py:948
  82.5 2.3 %place.1 = (bf16[512,768]{1,0:T(8,128)(2,1)}, bf16[512,768]{1,0:T(8,128)(2,1)}, f32[1,1]{1,0:T(1,128)}, f32[1,1]{1,0:T(1,128)}, f32[3,96,192]{2,1,0:T(8,128)}, /...) custom-call(bf16[512,768]{1,0:T(8,128)(2,1)S(1)} %get-tuple-element., ...), custom_call_target="tpu_custom_call" | custom-call | tf_op jit(solution)/shard_map/place/pallas_call | solution.py:1009

commit v3 on v2

--- a/solution.py
+++ b/solution.py
@@ -16,13 +16,18 @@
 SQRT_HALF = 0.7071067811865476
 PDF_SCALE = 0.3989422804014327
 VEC_ROWS = 16
+ORDERS = "ryyyyyryy"
 PLAN = (
-    "I_y", "fdS", "fdO", "fuS", "fuO", "ln1b0", "FD_11", "FD_10", "I_r", "FU_11",
-    "FU_10", "ln1b1", "dctx", "ab0", "ab1", "FD_01", "ab2", "FU_01", "ab3", "ab4",
-    "SD_1", "ab5", "dattT", "FD_00", "SU_1", "dsum", "fqS", "SD_0", "dtok0", "I_q",
-    "dtok1", "SU_0", "fqO", "qv", "V_y", "FU_00", "LD", "gtok0", "I_c", "FQ_11",
-    "pool", "LU", "V_r", "gtok1", "FQ_10", "FQ_01", "ED", "SQ_1", "FQ_00", "SQ_0",
-    "V_q", "EU", "LQ", "V_e", "EQ",
+    "fd", "FD0_11", "FD1_11", "FD0_10", "FD1_10", "FD0_01", "FD1_01", "FD0_00", "FD1_00", "fu",
+    "ln1b0", "I_y", "FD2_11", "FD2_10", "SD0_1", "SD1_1", "SD0_0", "SD1_0", "ln1b1", "dctx",
+    "ab0", "FD2_01", "ab1", "ab2", "FD2_00", "ab3", "ab4", "LD1", "FU0_11", "ab5",
+    "SD2_1", "dattT", "FU0_10", "I_r", "SD2_0", "FU0_01", "dsum", "LD0", "dtok0", "dtok1",
+    "FU0_00", "fq", "LD2", "FQ0_11", "FU1_11", "FQ0_10", "qv", "FU1_10", "FQ0_01", "FU1_01",
+    "FQ0_00", "SU0_1", "ED1", "FU1_00", "SU0_0", "I_q", "FU2_11", "V_y", "ED0", "SQ0_1",
+    "ED2", "SU1_1", "SQ0_0", "gtok0", "SU1_0", "FU2_10", "FU2_01", "LU0", "FU2_00", "SU2_1",
+    "FQ1_11", "gtok1", "FQ1_10", "LQ0", "FQ1_01", "V_r", "LU1", "FQ1_00", "SU2_0", "FQ2_11",
+    "I_c", "FQ2_10", "EU0", "LU2", "FQ2_01", "EQ0", "SQ1_1", "FQ2_00", "SQ1_0", "V_q",
+    "EU1", "SQ2_1", "EU2", "pool", "SQ2_0", "LQ1", "LQ2", "V_e", "EQ1", "EQ2",
 )
 VMEM_LIMIT = 56 * 1024 * 1024
 
@@ -126,28 +131,28 @@
 
 
 def remote_copy_count(pairs):
-    return 40 + 3 * (2 + 4 * pairs) + 4 * pairs
+    return 72 + 9 * 4 * pairs + 8 * pairs
 
 
 def layer_kernel(
     n_dp,
     tok_hbm,
     cot_hbm,
-    len_ref,
-    lab_ref,
+    len_hbm,
+    lab_hbm,
     wqkv_hbm,
-    qvb_ref,
+    qvb_hbm,
     wout_hbm,
-    bb_ref,
-    ng_ref,
-    ns_ref,
+    bb_hbm,
+    ng_hbm,
+    ns_hbm,
     wup_hbm,
-    upb_ref,
+    upb_hbm,
     wdn_hbm,
     wpool_hbm,
-    pb_ref,
-    wcls_ref,
-    cb_ref,
+    pb_hbm,
+    wcls_hbm,
+    cb_hbm,
     bout_out,
     gtok_out,
     gqkvo_out,
@@ -155,6 +160,16 @@
     gdn_out,
     gpool_out,
     vec_out,
+    len_ref,
+    lab_ref,
+    cb_ref,
+    qvb_ref,
+    bb_ref,
+    ng_ref,
+    ns_ref,
+    upb_ref,
+    pb_ref,
+    wcls_ref,
     tok,
     cot,
     wt,
@@ -162,6 +177,9 @@
     wup,
     wdn,
     wpool,
+    wup_tr,
+    wdn_tr,
+    wpool_tr,
     up_bias,
     bias_mask,
     k_pad,
@@ -185,7 +203,14 @@
     d_sec,
     d_br,
     d_br_tr,
+    d_br_peer,
     d_pre_low,
+    d_pre_peer,
+    act_peer,
+    hid_peer,
+    ctx_peer,
+    d_att_peer,
+    d_qkv_peer,
     d_first,
     d_att,
     d_att_tr,
@@ -194,10 +219,7 @@
     d_kv_send,
     d_kv_recv,
     d_qkv,
-    g_send,
-    g_recv,
-    g_own,
-    first_send,
+    g_low,
     first_recv,
     second_send,
     second_recv,
@@ -251,6 +273,8 @@
     shard = width // n_dp
     chunk = 128
     chunks = half // chunk
+    fine = 128
+    fines = half // fine
     tile = 256
     tiles = width // tile
     own_rows = pl.ds(pl.multiple_of(c * half, half), half)
@@ -263,14 +287,31 @@
 
     loads = Loads(load_sems)
     remote = Copies(send_sems, recv_sems)
+    load_len = loads.start(len_hbm, len_ref)
     load_tok = loads.start(tok_hbm, tok)
     load_wt = loads.start(wqkv_hbm, wt.at[c])
+    load_qvb = loads.start(qvb_hbm, qvb_ref)
+    load_upb = loads.start(upb_hbm, upb_ref)
+    load_lab = loads.start(lab_hbm, lab_ref)
+    load_small = [
+        loads.start(src, dst)
+        for src, dst in (
+            (cb_hbm, cb_ref),
+            (bb_hbm, bb_ref),
+            (ng_hbm, ng_ref),
+            (ns_hbm, ns_ref),
+            (pb_hbm, pb_ref),
+            (wcls_hbm, wcls_ref),
+        )
+    ]
     load_wo = loads.start(wout_hbm, wo.at[c])
     load_wup = loads.start(wup_hbm, wup.at[c])
     load_wdn = loads.start(wdn_hbm, wdn.at[c])
     load_pool = loads.start(wpool_hbm, wpool)
     load_cot = loads.start(cot_hbm.at[own_rows], cot)
 
+    load_len.wait()
+    load_lab.wait()
     lengths = [len_ref[0, i] for i in range(slots)]
     ends, total = [], 0
     for i in range(slots):
@@ -302,6 +343,7 @@
     for i in range(slots):
         first_row = first_row + jnp.where((lane_item == i) | (lane_item == i + slots), firsts[i], 0)
 
+    load_upb.wait()
     up_bias[c] = jnp.broadcast_to(upb_ref[...].astype(F32).reshape(1, width), (8, width))
     vec[...] = jnp.zeros_like(vec)
     pad_rows = q_pad.shape[1] - local_width
@@ -317,6 +359,7 @@
 
     load_tok.wait()
     load_wt.wait()
+    load_qvb.wait()
     rows_q, rows_k, rows_v = [slice(p * local_width, (p + 1) * local_width) for p in range(3)]
     query_bias = bias_cols(0, half)
     q_away[...] = (dot_nt(wt[c, rows_q, :], tok[away_rows, :]) + query_bias).astype(BF16)
@@ -367,18 +410,24 @@
     mark("attn_other")
     attend(1 - c)
     mark("out")
+    for load in load_small:
+        load.wait()
+    send_ctx = remote.start(ctx.at[1 - c], ctx_peer, core_dev)
     load_wo.wait()
     send_wo.wait_recv()
 
     def chunk_of(i):
         return slice(i * chunk, (i + 1) * chunk)
 
-    def exchange(which, i):
-        block = parts.at[which, x, chunk_of(i)]
+    def exchange(which, rows):
+        block = parts.at[which, x, rows]
         return remote.start(block, block, x_dev)
 
-    def both_parts(which, i):
-        return parts[which, 0, chunk_of(i), :].astype(F32) + parts[which, 1, chunk_of(i), :].astype(F32)
+    def fine_of(i):
+        return slice(i * fine, (i + 1) * fine)
+
+    def both_parts(which, rows):
+        return parts[which, 0, rows, :].astype(F32) + parts[which, 1, rows, :].astype(F32)
 
     ATT, FFN, HIDDEN, TOKEN = 0, 1, 2, 3
     send_att = []
@@ -386,7 +435,8 @@
         rows = chunk_of(i)
         partial_sum = dot_tn(ctx[0, :, rows], wo[0]) + dot_tn(ctx[1, :, rows], wo[1])
         parts[ATT, x, rows, :] = partial_sum.astype(BF16)
-        send_att.append(exchange(ATT, i))
+        for j in range(i * chunk // fine, (i + 1) * chunk // fine):
+            send_att.append(exchange(ATT, fine_of(j)))
     send_cnt_y.wait_recv()
     cnt_s[...] = cnt[...] + cnt_y[...]
     send_cnt_r = remote.start(cnt_s, cnt_r, r_dev)
@@ -395,23 +445,33 @@
     for b in range(2):
         k_tr[b] = jnp.transpose(k_pad[b])[0:local_width, :]
         v_pad[b, :, 0:local_width] = jnp.transpose(v_tr[b])
-    tok_tr[...] = jnp.transpose(tok[own_rows, :])
-
-    mark("ffn_f")
+    tok_tr[0] = jnp.transpose(tok[own_rows, :])
+    tok_tr[1] = jnp.transpose(tok[away_rows, :])
+
     load_wup.wait()
     load_wdn.wait()
-    send_ffn = []
-    for i in range(chunks):
-        rows = chunk_of(i)
+    load_pool.wait()
+    wpool_tr[...] = jnp.transpose(wpool[...])
+    send_wup.wait_recv()
+    send_wdn.wait_recv()
+    for b in range(2):
+        wup_tr[b] = jnp.transpose(wup[b])
+        wdn_tr[b] = jnp.transpose(wdn[b])
+
+    mark("ffn_f")
+    send_ffn, send_hid, send_act = [], [], []
+    for i in range(fines):
+        rows = fine_of(i)
         send_att[i].wait_recv()
-        token_rows = pl.ds(pl.multiple_of(c * half + i * chunk, chunk), chunk)
-        attention = both_parts(ATT, i) + bb_ref[0:1, :]
+        token_rows = pl.ds(pl.multiple_of(c * half + i * fine, fine), fine)
+        attention = both_parts(ATT, rows) + bb_ref[0:1, :]
         normed, inv_scale = norm_forward(tok[token_rows, :].astype(F32) + attention)
         n_one[rows, :] = normed
         scale_one[rows, :] = inv_scale
         value = normed * ng_ref[0:1, :] + ns_ref[0:1, :]
         hid[rows, :] = value
         hid_low[rows, :] = value.astype(BF16)
+        send_hid.append(remote.start(hid_low.at[rows], hid_peer.at[rows], core_dev))
         for b in range(2):
             core = c if b == 0 else 1 - c
             if i == 0 and b == 1:
@@ -427,18 +487,21 @@
                 send_wdn.wait_recv()
             product = dot_nn(act_low[b, rows, :], wdn[core])
             if b == 0:
-                acc[...] = product
+                acc[0:fine, :] = product
             else:
-                parts[FFN, x, rows, :] = (acc[...] + product).astype(BF16)
-        send_ffn.append(exchange(FFN, i))
+                parts[FFN, x, rows, :] = (acc[0:fine, :] + product).astype(BF16)
+        send_ffn.append(exchange(FFN, rows))
+        send_act.append(remote.start(act_low.at[1, rows], act_peer.at[rows], core_dev))
         if i == 0:
             send_cnt_r.wait_recv()
             cnt_q[q] = cnt_s[...] + cnt_r[...]
             send_cnt_q = [remote.start(cnt_q.at[q], cnt_q.at[q], q_dev(k)) for k in away]
 
     mark("hid_tr")
-    hid_tr[...] = jnp.transpose(hid_low[...])
-    load_pool.wait()
+    hid_tr[0] = jnp.transpose(hid_low[...])
+    for copy in send_hid:
+        copy.wait_recv()
+    hid_tr[1] = jnp.transpose(hid_peer[...])
     load_cot.wait()
     for copy in send_cnt_q:
         copy.wait_recv()
@@ -462,12 +525,13 @@
 
     mark("ln2")
     up_sums = [[None] * tiles, [None] * tiles]
-    send_hidden = []
+    send_hidden, send_br, send_pre = [], [], []
     for i in range(chunks):
         rows = chunk_of(i)
         place = c * half + i * chunk
-        send_ffn[i].wait_recv()
-        normed, inv_scale = norm_forward(hid[rows, :] + (both_parts(FFN, i) + bb_ref[1:2, :]))
+        for j in range(i * chunk // fine, (i + 1) * chunk // fine):
+            send_ffn[j].wait_recv()
+        normed, inv_scale = norm_forward(hid[rows, :] + (both_parts(FFN, rows) + bb_ref[1:2, :]))
         low = (normed * ng_ref[1:2, :] + ns_ref[1:2, :]).astype(BF16)
         bout_out[pl.ds(pl.multiple_of(place, chunk), chunk), :] = low
 
@@ -502,7 +566,7 @@
             items[1] += d_pre
         if i == chunks - 1:
             send_items = remote.start(items.at[1 - c], items_c, core_dev)
-        d_picked = dot_nt(d_pre, wpool[...])
+        d_picked = dot_nn(d_pre, wpool_tr[...])
         d_high = d_picked.astype(BF16)
         d_both = jnp.concatenate([d_high, (d_picked - d_high.astype(F32)).astype(BF16)], axis=0)
 
@@ -516,68 +580,57 @@
         add_rows(1, col_sum(d_second))
         d_sec[rows, :] = d_second
         d_br[rows, :] = d_second.astype(BF16)
+        send_br.append(remote.start(d_br.at[rows], d_br_peer.at[rows], core_dev))
         for b in range(2):
             core = c if b == 0 else 1 - c
             for n in range(tiles):
                 cols = slice(n * tile, (n + 1) * tile)
-                d_act = dot_nt(d_br[rows, :], wdn[core, cols, :])
+                d_act = dot_nn(d_br[rows, :], wdn_tr[core, :, cols])
                 low = (d_act * d_gelu[b, rows, cols]).astype(BF16)
                 d_pre_low[b, rows, cols] = low
                 up_sum = col_sum(low.astype(F32))
                 up_sums[b][n] = up_sum if i == 0 else up_sums[b][n] + up_sum
-            product = dot_nt(d_pre_low[b, rows, :], wup[core])
+            product = dot_nn(d_pre_low[b, rows, :], wup_tr[core])
             if b == 0:
                 acc[...] = product
             else:
                 parts[HIDDEN, x, rows, :] = (acc[...] + product).astype(BF16)
-        send_hidden.append(exchange(HIDDEN, i))
+        send_hidden.append(exchange(HIDDEN, rows))
+        send_pre.append(remote.start(d_pre_low.at[1, rows], d_pre_peer.at[rows], core_dev))
     vec[pl.ds(11 + c, 1), :] = jnp.concatenate(up_sums[0], axis=1)
     vec[pl.ds(12 - c, 1), :] = jnp.concatenate(up_sums[1], axis=1)
     send_out = remote.start(bout_out.at[own_rows], bout_out.at[own_rows], core_dev)
 
-    DOWN, UP, QKVO = 0, 1, 2
-    along = {DOWN: (r, y, r_dev, y_dev), UP: (y, r, y_dev, r_dev), QKVO: (y, r, y_dev, r_dev)}
-    row_major = {DOWN: True, UP: False, QKVO: False}
+    DOWN, UP, QKVO = 0, tiles, 2 * tiles
+    y_first, r_first = (y, r, y_dev, r_dev), (r, y, r_dev, y_dev)
+    along = [y_first if letter == "y" else r_first for letter in ORDERS]
+    row_major = [letter == "r" for letter in ORDERS]
     reach = {1: list(away), 0: [0]}
     slot_of = {(flip, k): (1 - flip) * pairs + (k - 1) % pairs for flip in range(2) for k in range(pairs)}
     sent = {}
     step = {}
 
-    def store_blocks(out, block, cols, product):
+    def store_blocks(block, product):
         for j in range(n_dp):
-            value = product[j * shard : (j + 1) * shard, :].astype(out.dtype)
             bits = (j % 2, (j // 2) % 2)
             if row_major[block]:
                 bits = bits[::-1]
-            out[block, bits[0], bits[1], j // 4, :, cols] = value
-
-    def fill(out, block, product_of):
+            g_low[block, bits[0], bits[1], j // 4] = product[j * shard : (j + 1) * shard, :].astype(BF16)
+
+    def fill(block, product_of):
         for n in range(tiles):
-            cols = slice(n * tile, (n + 1) * tile)
-            store_blocks(out, block, cols, product_of(cols))
-
-    def core_send(block):
-        first = along[block][0]
-        for name, side in (("away", 1 - first), ("kept", first)):
-            sent[block, name] = remote.start(g_send.at[block, side], g_recv.at[block, side], core_dev)
-
-    def after_core(block, name, first_value, second_value, q_index):
-        sent[block, name].wait_recv()
-        index = (block, first_value, second_value, q_index)
-        return g_own[index] + g_recv[index].astype(F32)
+            store_blocks(block + n, product_of(slice(n * tile, (n + 1) * tile)))
 
     def first_step(block, flip, group):
         first, second, device, _ = along[block]
         for k in reach[group]:
-            slot = slot_of[flip, k]
-            value = after_core(block, "away", 1 - first, 1 - second if flip else second, q_of(k))
-            first_send[block, slot] = value.astype(BF16)
-            sent[block, 1, flip, k] = remote.start(first_send.at[block, slot], first_recv.at[block, slot], device)
+            source = g_low.at[block, 1 - first, 1 - second if flip else second, q_of(k)]
+            sent[block, 1, flip, k] = remote.start(source, first_recv.at[block, slot_of[flip, k]], device)
 
     def first_sum(block, flip, k):
         first, second, _, _ = along[block]
         sent[block, 1, flip, k].wait_recv()
-        value = after_core(block, "kept", first, 1 - second if flip else second, q_of(k))
+        value = g_low[block, first, 1 - second if flip else second, q_of(k)].astype(F32)
         return value + first_recv[block, slot_of[flip, k]].astype(F32)
 
     def second_step(block, group):
@@ -599,29 +652,33 @@
         for k in away:
             sent[block, 3, k].wait_recv()
             result = result + last_recv[block, k - 1].astype(F32)
-        out[...] = result
-
-    for letter, block, out in (("D", DOWN, gdn_out), ("U", UP, gup_out), ("Q", QKVO, gqkvo_out)):
-        for group in range(2):
-            for flip in range(2):
-                step["F%s_%d%d" % (letter, flip, group)] = partial(first_step, block, flip, group)
-            step["S%s_%d" % (letter, group)] = partial(second_step, block, group)
-        step["L" + letter] = partial(last_step, block)
-        step["E" + letter] = partial(end_step, block, out)
-
-    def fill_down_send():
-        d_br_tr[...] = jnp.transpose(d_br[...])
-        fill(g_send, DOWN, lambda cols: dot_nn(d_br_tr[...], act_low[1, :, cols]))
-        core_send(DOWN)
-
-    def fill_up_send():
-        fill(g_send, UP, lambda cols: dot_nn(hid_tr[...], d_pre_low[1, :, cols]))
-        core_send(UP)
-
-    step["fdS"] = fill_down_send
-    step["fdO"] = lambda: fill(g_own, DOWN, lambda cols: dot_nn(d_br_tr[...], act_low[0, :, cols]))
-    step["fuS"] = fill_up_send
-    step["fuO"] = lambda: fill(g_own, UP, lambda cols: dot_nn(hid_tr[...], d_pre_low[0, :, cols]))
+        n = block % tiles
+        out[:, n * tile : (n + 1) * tile] = result
+
+    for letter, first_block, out in (("D", DOWN, gdn_out), ("U", UP, gup_out), ("Q", QKVO, gqkvo_out)):
+        for n in range(tiles):
+            block, name = first_block + n, letter + str(n)
+            for group in range(2):
+                for flip in range(2):
+                    step["F%s_%d%d" % (name, flip, group)] = partial(first_step, block, flip, group)
+                step["S%s_%d" % (name, group)] = partial(second_step, block, group)
+            step["L" + name] = partial(last_step, block)
+            step["E" + name] = partial(end_step, block, out)
+
+    def fill_down():
+        d_br_tr[0] = jnp.transpose(d_br[...])
+        for copy in send_br + send_act:
+            copy.wait_recv()
+        d_br_tr[1] = jnp.transpose(d_br_peer[...])
+        fill(DOWN, lambda cols: dot_nn(d_br_tr[0], act_low[0, :, cols]) + dot_nn(d_br_tr[1], act_peer[:, cols]))
+
+    def fill_up():
+        for copy in send_pre:
+            copy.wait_recv()
+        fill(UP, lambda cols: dot_nn(hid_tr[0], d_pre_low[0, :, cols]) + dot_nn(hid_tr[1], d_pre_peer[:, cols]))
+
+    step["fd"] = fill_down
+    step["fu"] = fill_up
 
     def item_rows(first, count):
         return pl.ds(pl.multiple_of(first * slots, count * slots), count * slots)
@@ -660,7 +717,7 @@
     def norm_one_back(i):
         rows = chunk_of(i)
         send_hidden[i].wait_recv()
-        d_hidden = both_parts(HIDDEN, i) + d_sec[rows, :]
+        d_hidden = both_parts(HIDDEN, rows) + d_sec[rows, :]
         normed = n_one[rows, :]
         add_rows(2, col_sum(d_hidden * normed))
         add_rows(4, col_sum(d_hidden))
@@ -668,6 +725,7 @@
         add_rows(0, col_sum(gradient))
         d_first[rows, :] = gradient
         d_att[rows, :] = gradient.astype(BF16)
+        sent["d_att", i] = remote.start(d_att.at[rows], d_att_peer.at[rows], core_dev)
 
     def context_back():
         for b in range(2):
@@ -694,12 +752,16 @@
             sent["kv"] = remote.start(d_kv_send.at[1 - c], d_kv_recv, core_dev)
 
     def turn_attention():
-        d_att_tr[...] = jnp.transpose(d_att[...])
+        d_att_tr[0] = jnp.transpose(d_att[...])
+        for i in range(chunks):
+            sent["d_att", i].wait_recv()
+        d_att_tr[1] = jnp.transpose(d_att_peer[...])
 
     def join_cores():
         sent["kv"].wait_recv()
         for b in range(2):
             d_qkv[b, local_width:, :] = (d_kv_f32[c, b] + d_kv_recv[b].astype(F32)).astype(BF16)
+        sent["d_qkv"] = remote.start(d_qkv.at[1 - c], d_qkv_peer, core_dev)
 
     for i in range(chunks):
         step["ln1b%d" % i] = partial(norm_one_back, i)
@@ -709,32 +771,30 @@
     step["dattT"] = turn_attention
     step["dsum"] = join_cores
 
-    def fill_qkvo(core, out):
-        first_part = dot_nt(tok_tr[...], d_qkv[core])
-        second_part = dot_nt(d_att_tr[...], ctx[core])
-        store_blocks(out, QKVO, slice(0, width), jnp.concatenate([first_part, second_part], axis=1))
-
-    def fill_qkvo_send():
-        fill_qkvo(1 - c, g_send)
-        core_send(QKVO)
+    def fill_qkvo():
+        sent["d_qkv"].wait_recv()
+        send_ctx.wait_recv()
+        first_part = dot_nt(tok_tr[0], d_qkv[c]) + dot_nt(tok_tr[1], d_qkv_peer[...])
+        second_part = dot_nt(d_att_tr[0], ctx[c]) + dot_nt(d_att_tr[1], ctx_peer[...])
+        both = jnp.concatenate([first_part, second_part], axis=1)
+        fill(QKVO, lambda cols: both[:, cols])
 
     def token_part(i):
         send_wt.wait_recv()
         rows = chunk_of(i)
         partial_sum = dot_tn(d_qkv[0, :, rows], wt[0]) + dot_tn(d_qkv[1, :, rows], wt[1])
         parts[TOKEN, x, rows, :] = partial_sum.astype(BF16)
-        sent["token", i] = exchange(TOKEN, i)
+        sent["token", i] = exchange(TOKEN, rows)
 
     def token_end(i):
         sent["token", i].wait_recv()
         rows = chunk_of(i)
         place = pl.ds(pl.multiple_of(c * half + i * chunk, chunk), chunk)
-        gtok_out[place, :] = (both_parts(TOKEN, i) + d_first[rows, :]).astype(BF16)
+        gtok_out[place, :] = (both_parts(TOKEN, rows) + d_first[rows, :]).astype(BF16)
         if i == chunks - 1:
             sent["gtok"] = remote.start(gtok_out.at[own_rows], gtok_out.at[own_rows], core_dev)
 
-    step["fqS"] = fill_qkvo_send
-    step["fqO"] = lambda: fill_qkvo(c, g_own)
+    step["fq"] = fill_qkvo
     for i in range(chunks):
         step["dtok%d" % i] = partial(token_part, i)
         step["gtok%d" % i] = partial(token_end, i)
@@ -790,8 +850,23 @@
     gdn_in,
     gpool_in,
     vec_in,
-    bout,
-    gtok,
+    bout_out,
+    gtok_out,
+    loss_out,
+    entropy_out,
+    gqkv_out,
+    gqv_out,
+    gout_out,
+    gbranch_out,
+    ggain_out,
+    gshift_out,
+    gup_out,
+    gupb_out,
+    gdn_out,
+    gpool_out,
+    gpoolb_out,
+    gclass_out,
+    gclassb_out,
     loss,
     entropy,
     gqkv,
@@ -800,19 +875,22 @@
     gbranch,
     ggain,
     gshift,
-    gup,
     gupb,
-    gdn,
-    gpool,
     gpoolb,
     gclass,
     gclassb,
     sems,
 ):
-    moves = ((bout_in, bout), (gtok_in, gtok), (gup_in, gup), (gdn_in, gdn), (gpool_in, gpool))
-    copies = [pltpu.make_async_copy(src, dst, sems.at[i]) for i, (src, dst) in enumerate(moves)]
-    for copy in copies:
+    moves = ((bout_in, bout_out), (gtok_in, gtok_out), (gup_in, gup_out), (gdn_in, gdn_out), (gpool_in, gpool_out))
+    copies = []
+
+    def send(src, dst):
+        copy = pltpu.make_async_copy(src, dst, sems.at[len(copies)])
         copy.start()
+        copies.append(copy)
+
+    for src, dst in moves:
+        send(src, dst)
     dp = lax.axis_index("dp")
     c = lax.rem(lax.axis_index("tensor"), 2)
     width = vec_in.shape[1]
@@ -820,7 +898,9 @@
     local_width = gout.shape[0]
     for part in range(3):
         gqkv[part] = gqkvo_in[:, part * local_width : (part + 1) * local_width]
+    send(gqkv, gqkv_out)
     gout[...] = jnp.transpose(gqkvo_in[:, 3 * local_width :])
+    send(gout, gout_out)
     sums = vec_in[...]
     mine = pltpu.roll(sums, lax.rem(width - dp * shard, width), axis=1)
     gbranch[...] = mine[0:2, :shard]
@@ -837,6 +917,20 @@
     loss[...] = sums[10:11, 0:1] * inv_count
     entropy[...] = sums[10:11, 1:2] * inv_count
     gclassb[...] = sums[10:11, 128 : 128 + gclassb.shape[1]]
+    small_moves = (
+        (loss, loss_out),
+        (entropy, entropy_out),
+        (gqv, gqv_out),
+        (gbranch, gbranch_out),
+        (ggain, ggain_out),
+        (gshift, gshift_out),
+        (gupb, gupb_out),
+        (gpoolb, gpoolb_out),
+        (gclass, gclass_out),
+        (gclassb, gclassb_out),
+    )
+    for src, dst in small_moves:
+        send(src, dst)
     for copy in copies:
         copy.wait()
 
@@ -875,11 +969,22 @@
     shape = jax.ShapeDtypeStruct
     anywhere = pl.BlockSpec(memory_space=pl.ANY)
     vmem = pl.BlockSpec(memory_space=pltpu.VMEM)
-    smem = pl.BlockSpec(memory_space=pltpu.SMEM)
-    blocks = (3, 2, 2, pairs, shard, width)
+    pieces = 3 * width // 256
+    blocks = (pieces, 2, 2, pairs, shard, 256)
     copies = remote_copy_count(pairs)
     V = pltpu.VMEM
+    S = pltpu.SMEM
     scratch = dict(
+        len_ref=S(lengths.shape, jnp.int32),
+        lab_ref=S(labels.shape, jnp.int32),
+        cb_ref=S((1, classes), F32),
+        qvb_ref=V(qv_bias.shape, F32),
+        bb_ref=V(branch_bias.shape, F32),
+        ng_ref=V(norm_gain.shape, F32),
+        ns_ref=V(norm_shift.shape, F32),
+        upb_ref=V(up_bias.shape, BF16),
+        pb_ref=V(pool_bias.shape, F32),
+        wcls_ref=V((classes, width), BF16),
         tok=V((token_count, width), BF16),
         cot=V((half, width), BF16),
         wt=V((2, 3 * local_width, width), BF16),
@@ -887,6 +992,9 @@
         wup=V((2, width, hidden), BF16),
         wdn=V((2, hidden, width), BF16),
         wpool=V((width, width), BF16),
+        wup_tr=V((2, hidden, width), BF16),
+        wdn_tr=V((2, width, hidden), BF16),
+        wpool_tr=V((width, width), BF16),
         up_bias=V((2, 8, width), F32),
         bias_mask=V((token_count, half), F32),
         k_pad=V((2, token_count, padded), BF16),
@@ -899,8 +1007,8 @@
         ctx=V((2, local_width, half), BF16),
         hid=V((half, width), F32),
         hid_low=V((half, width), BF16),
-        hid_tr=V((width, half), BF16),
-        tok_tr=V((width, half), BF16),
+        hid_tr=V((2, width, half), BF16),
+        tok_tr=V((2, width, half), BF16),
         n_one=V((half, width), F32),
         scale_one=V((half, 1), F32),
         act_low=V((2, half, hidden), BF16),
@@ -909,25 +1017,29 @@
         parts=V((4, 2, half, width), BF16),
         d_sec=V((half, width), F32),
         d_br=V((half, width), BF16),
-        d_br_tr=V((width, half), BF16),
+        d_br_tr=V((2, width, half), BF16),
+        d_br_peer=V((half, width), BF16),
         d_pre_low=V((2, half, hidden), BF16),
+        d_pre_peer=V((half, hidden), BF16),
+        act_peer=V((half, hidden), BF16),
+        hid_peer=V((half, width), BF16),
+        ctx_peer=V((local_width, half), BF16),
+        d_att_peer=V((half, width), BF16),
+        d_qkv_peer=V((3 * local_width, half), BF16),
         d_first=V((half, width), F32),
         d_att=V((half, width), BF16),
-        d_att_tr=V((width, half), BF16),
+        d_att_tr=V((2, width, half), BF16),
         d_ctx=V((2, padded, half), BF16),
         d_kv_f32=V((2, 2, 2 * local_width, half), F32),
         d_kv_send=V((2, 2, 2 * local_width, half), BF16),
         d_kv_recv=V((2, 2 * local_width, half), BF16),
         d_qkv=V((2, 3 * local_width, half), BF16),
-        g_send=V(blocks, BF16),
-        g_recv=V(blocks, BF16),
-        g_own=V(blocks, F32),
-        first_send=V((3, 2 * pairs, shard, width), BF16),
-        first_recv=V((3, 2 * pairs, shard, width), BF16),
-        second_send=V((3, pairs, shard, width), BF16),
-        second_recv=V((3, pairs, shard, width), BF16),
-        last_send=V((3, pairs - 1, shard, width), BF16),
-        last_recv=V((3, pairs - 1, shard, width), BF16),
+        g_low=V(blocks, BF16),
+        first_recv=V((pieces, 2 * pairs, shard, 256), BF16),
+        second_send=V((pieces, pairs, shard, 256), BF16),
+        second_recv=V((pieces, pairs, shard, 256), BF16),
+        last_send=V((pieces, pairs - 1, shard, 256), BF16),
+        last_recv=V((pieces, pairs - 1, shard, 256), BF16),
         pool_fin=V((width, width), F32),
         items=V((2, slots, width), BF16),
         items_c=V((slots, width), BF16),
@@ -956,29 +1068,11 @@
             V((shard, width), F32),
             V((VEC_ROWS, width), F32),
         ],
-        in_specs=[
-            anywhere,
-            anywhere,
-            smem,
-            smem,
-            anywhere,
-            vmem,
-            anywhere,
-            vmem,
-            vmem,
-            vmem,
-            anywhere,
-            vmem,
-            anywhere,
-            anywhere,
-            vmem,
-            vmem,
-            smem,
-        ],
+        in_specs=[anywhere] * 17,
         out_specs=[vmem] * 7,
         scratch_shapes=list(scratch.values())
         + [
-            pltpu.SemaphoreType.DMA((8,)),
+            pltpu.SemaphoreType.DMA((20,)),
             pltpu.SemaphoreType.DMA((copies,)),
             pltpu.SemaphoreType.DMA((copies,)),
         ],
@@ -1006,30 +1100,32 @@
         class_bias.reshape(1, classes),
     )
     small = local_width // n_dp
+    outputs = [
+        shape((token_count, width), BF16),
+        shape((token_count, width), BF16),
+        shape((1, 1), F32),
+        shape((1, 1), F32),
+        shape((3, shard, local_width), F32),
+        shape((2, small), F32),
+        shape((local_width, shard), F32),
+        shape((2, shard), F32),
+        shape((2, shard), F32),
+        shape((2, shard), F32),
+        shape((shard, hidden), F32),
+        shape((1, hidden // n_dp), F32),
+        shape((shard, hidden), F32),
+        shape((shard, width), F32),
+        shape((1, shard), F32),
+        shape((classes, shard), F32),
+        shape((1, classes), F32),
+    ]
+    held = [out for i, out in enumerate(outputs) if i not in (0, 1, 10, 12, 13)]
     placed = pl.pallas_call(
         partial(place_kernel, n_dp),
-        out_shape=[
-            shape((token_count, width), BF16),
-            shape((token_count, width), BF16),
-            shape((1, 1), F32),
-            shape((1, 1), F32),
-            shape((3, shard, local_width), F32),
-            shape((2, small), F32),
-            shape((local_width, shard), F32),
-            shape((2, shard), F32),
-            shape((2, shard), F32),
-            shape((2, shard), F32),
-            shape((shard, hidden), F32),
-            shape((1, hidden // n_dp), F32),
-            shape((shard, hidden), F32),
-            shape((shard, width), F32),
-            shape((1, shard), F32),
-            shape((classes, shard), F32),
-            shape((1, classes), F32),
-        ],
+        out_shape=outputs,
         in_specs=[vmem] * 7,
-        out_specs=[anywhere] * 2 + [vmem] * 8 + [anywhere, vmem, anywhere, anywhere] + [vmem] * 3,
-        scratch_shapes=[pltpu.SemaphoreType.DMA((5,))],
+        out_specs=[anywhere] * 17,
+        scratch_shapes=[V(out.shape, out.dtype) for out in held] + [pltpu.SemaphoreType.DMA((17,))],
         name="place",
     )(*[pltpu.with_memory_space_constraint(value, pltpu.VMEM) for value in found])
     (

time: 85.2 us -> 81.9 us (0.961)
  Pallas kernels: 84.1 us -> 80.9 us
    pallas_call x1, Pallas kernels: 81.8 us -> 79.2 us  [on_device(): pl.pallas_call(partial(layer_kernel, n_dp), out_shape=[V((token_count, wi...]
where the time goes in v3:
time: 81.9 us; the launch traced here: 81.8 us
  Pallas kernels  80.9 us (99%)
  between operations  0.83 us (1%)
    pallas_call x1, Pallas kernels, on_device(): pl.pallas_call(partial(layer_kernel, n_dp), out_shape=[V((token_count, wi...  79.2 us
    pallas_call x1, Pallas kernels, on_device(): pl.pallas_call(partial(place_kernel, n_dp), out_shape=outputs, in_specs=[...  1.77 us

profile of v3, /device:TPU:0, one launch (start us, length us, event | category | flops | bytes accessed | tf_op | source)
XLA Modules:
  0.0 81.8 jit_solution(1855082103235637690)
XLA Ops:
  0.7 79.2 %layer.1 = (bf16[512,768]{1,0:T(8,128)(2,1)S(1)}, bf16[512,768]{1,0:T(8,128)(2,1)S(1)}, f32[96,768]{1,0:T(8,128)S(1)}, f32[96,768]{1,0:T(8,128)S(1)}, f32[96,768...) custom-call(bf16[512,768]{1,0:T(8,128)(2,1)} %tok_hbm.1, bf16[512,768]{1,0:T(8,128)(2,1)} %cot_hbm.1, ...), custom_call_target="tpu_custom_call" | custom-call | tf_op jit(solution)/shard_map/layer/pallas_call | solution.py:1060
  79.8 1.8 %place.1 = (bf16[512,768]{1,0:T(8,128)(2,1)}, bf16[512,768]{1,0:T(8,128)(2,1)}, f32[1,1]{1,0:T(1,128)}, f32[1,1]{1,0:T(1,128)}, f32[3,96,192]{2,1,0:T(8,128)}, /...) custom-call(bf16[512,768]{1,0:T(8,128)(2,1)S(1)} %get-tuple-element., ...), custom_call_target="tpu_custom_call" | custom-call | tf_op jit(solution)/shard_map/place/pallas_call | solution.py:1123

commit v4 on v3

--- a/solution.py
+++ b/solution.py
@@ -16,18 +16,19 @@
 SQRT_HALF = 0.7071067811865476
 PDF_SCALE = 0.3989422804014327
 VEC_ROWS = 16
-ORDERS = "ryyyyyryy"
+ORDERS = "yyryyrryy"
 PLAN = (
-    "fd", "FD0_11", "FD1_11", "FD0_10", "FD1_10", "FD0_01", "FD1_01", "FD0_00", "FD1_00", "fu",
-    "ln1b0", "I_y", "FD2_11", "FD2_10", "SD0_1", "SD1_1", "SD0_0", "SD1_0", "ln1b1", "dctx",
-    "ab0", "FD2_01", "ab1", "ab2", "FD2_00", "ab3", "ab4", "LD1", "FU0_11", "ab5",
-    "SD2_1", "dattT", "FU0_10", "I_r", "SD2_0", "FU0_01", "dsum", "LD0", "dtok0", "dtok1",
-    "FU0_00", "fq", "LD2", "FQ0_11", "FU1_11", "FQ0_10", "qv", "FU1_10", "FQ0_01", "FU1_01",
-    "FQ0_00", "SU0_1", "ED1", "FU1_00", "SU0_0", "I_q", "FU2_11", "V_y", "ED0", "SQ0_1",
-    "ED2", "SU1_1", "SQ0_0", "gtok0", "SU1_0", "FU2_10", "FU2_01", "LU0", "FU2_00", "SU2_1",
-    "FQ1_11", "gtok1", "FQ1_10", "LQ0", "FQ1_01", "V_r", "LU1", "FQ1_00", "SU2_0", "FQ2_11",
-    "I_c", "FQ2_10", "EU0", "LU2", "FQ2_01", "EQ0", "SQ1_1", "FQ2_00", "SQ1_0", "V_q",
-    "EU1", "SQ2_1", "EU2", "pool", "SQ2_0", "LQ1", "LQ2", "V_e", "EQ1", "EQ2",
+    "fd0", "FD0_11", "FD0_10", "fd1", "fd2", "FD2_11", "FD2_10", "FD1_11", "fu0", "fu1",
+    "FD2_01", "fu2", "ln1b0", "I_y", "FD1_10", "FD2_00", "FD1_01", "FU2_11", "SD0_1", "FD1_00",
+    "SD2_1", "SD0_0", "SD2_0", "ln1b1", "SD1_1", "dctx", "ab0", "ab1", "FU1_11", "SD1_0",
+    "ab2", "ab3", "I_r", "FU1_10", "ab4", "SU2_1", "ab5", "FU2_10", "dattT", "LD2",
+    "FU1_01", "dsum", "FU2_01", "dtok0", "LD1", "FU1_00", "dtok1", "SU1_1", "FU0_11", "fq",
+    "SU1_0", "FQ1_11", "qv", "SU2_0", "I_q", "ED2", "FQ1_10", "LU2", "FQ1_01", "V_y",
+    "SU0_1", "FQ1_00", "LU1", "SQ1_1", "FU0_10", "ED1", "FU0_01", "gtok0", "FQ0_11", "SQ1_0",
+    "FU0_00", "I_x", "FD0_01", "FQ0_10", "FD0_00", "FQ0_01", "V_r", "SU0_0", "FQ2_11", "LQ1",
+    "gtok1", "LU0", "FQ2_10", "SQ0_1", "EU1", "LD0", "FQ2_01", "SQ0_0", "SQ2_1", "EQ1",
+    "FQ2_00", "SQ2_0", "V_q", "LQ0", "I_c", "FQ0_00", "EU0", "FU2_00", "LQ2", "ED0",
+    "V_e", "EQ0", "pool", "EU2", "EQ2",
 )
 VMEM_LIMIT = 56 * 1024 * 1024
 
@@ -665,26 +666,31 @@
             step["L" + name] = partial(last_step, block)
             step["E" + name] = partial(end_step, block, out)
 
-    def fill_down():
-        d_br_tr[0] = jnp.transpose(d_br[...])
-        for copy in send_br + send_act:
-            copy.wait_recv()
-        d_br_tr[1] = jnp.transpose(d_br_peer[...])
-        fill(DOWN, lambda cols: dot_nn(d_br_tr[0], act_low[0, :, cols]) + dot_nn(d_br_tr[1], act_peer[:, cols]))
-
-    def fill_up():
+    def fill_down(n):
+        if n == 0:
+            d_br_tr[0] = jnp.transpose(d_br[...])
+            for copy in send_br + send_act:
+                copy.wait_recv()
+            d_br_tr[1] = jnp.transpose(d_br_peer[...])
+        cols = slice(n * tile, (n + 1) * tile)
+        store_blocks(DOWN + n, dot_nn(d_br_tr[0], act_low[0, :, cols]) + dot_nn(d_br_tr[1], act_peer[:, cols]))
+
+    def fill_up(n):
         for copy in send_pre:
             copy.wait_recv()
-        fill(UP, lambda cols: dot_nn(hid_tr[0], d_pre_low[0, :, cols]) + dot_nn(hid_tr[1], d_pre_peer[:, cols]))
-
-    step["fd"] = fill_down
-    step["fu"] = fill_up
+        cols = slice(n * tile, (n + 1) * tile)
+        store_blocks(UP + n, dot_nn(hid_tr[0], d_pre_low[0, :, cols]) + dot_nn(hid_tr[1], d_pre_peer[:, cols]))
+
+    for n in range(tiles):
+        step["fd%d" % n] = partial(fill_down, n)
+        step["fu%d" % n] = partial(fill_up, n)
 
     def item_rows(first, count):
         return pl.ds(pl.multiple_of(first * slots, count * slots), count * slots)
 
     def pass_items(name, rows, devices):
-        sent[name] = [remote.start(item_all.at[c, rows], item_all.at[c, rows], device) for device in devices]
+        block = item_all.at[c, x, rows]
+        sent[name] = [remote.start(block, block, device) for device in devices]
 
     def settle(name):
         for copy in sent[name]:
@@ -692,7 +698,8 @@
 
     def items_y():
         send_items.wait_recv()
-        item_all[c, item_rows(dp, 1), :] = items[c] + items_c[...]
+        both = items[c] + items_c[...]
+        item_all[c, x, item_rows(dp, 1), :] = jnp.where(x == 0, both[:, : width // 2], both[:, width // 2 :])
         pass_items("items_y", item_rows(dp, 1), [y_dev])
 
     def items_r():
@@ -703,16 +710,21 @@
         settle("items_r")
         pass_items("items_q", item_rows(q * 4, 4), [q_dev(k) for k in away])
 
+    def items_x():
+        settle("items_q")
+        sent["items_x"] = [remote.start(item_all.at[c, x], item_all.at[c, x], x_dev)]
+
     def items_core():
-        settle("items_q")
+        settle("items_x")
         sent["items_core"] = [remote.start(item_all.at[c], item_all.at[c], core_dev)]
 
     def pool():
         settle("items_core")
-        pool_fin[...] = dot_tn(item_all[0], item_all[1])
+        picked_all, d_pre_all = [jnp.concatenate([item_all[p, 0], item_all[p, 1]], axis=1) for p in range(2)]
+        pool_fin[...] = dot_tn(picked_all, d_pre_all)
         gpool_out[...] = pool_fin[pl.ds(pl.multiple_of(dp * shard, 8), shard), :]
 
-    step.update(I_y=items_y, I_r=items_r, I_q=items_q, I_c=items_core, pool=pool)
+    step.update(I_y=items_y, I_r=items_r, I_q=items_q, I_x=items_x, I_c=items_core, pool=pool)
 
     def norm_one_back(i):
         rows = chunk_of(i)
@@ -799,17 +811,20 @@
         step["dtok%d" % i] = partial(token_part, i)
         step["gtok%d" % i] = partial(token_end, i)
 
+    def vec_rows(core):
+        return pl.ds(pl.multiple_of(core * VEC_ROWS // 2, VEC_ROWS // 2), VEC_ROWS // 2)
+
     def vec_core():
         ones = jnp.ones((8, half), BF16)
         sums = [dot_nt(ones, d_qkv[b])[0:1, :] for b in range(2)]
         columns = [v[:, :local_width] for v in sums] + [v[:, 2 * local_width :] for v in sums]
         vec[13:14, :] = jnp.concatenate(columns, axis=1)
         vec[14:15, 0:128] = item_count[0:1, :]
-        sent["vec"] = remote.start(vec, vec_c, core_dev)
+        sent["vec"] = remote.start(vec.at[vec_rows(1 - c)], vec_c, core_dev)
 
     def vec_along_y():
         sent["vec"].wait_recv()
-        vec_s[...] = vec[...] + vec_c[...]
+        vec_s[...] = vec[vec_rows(c), :] + vec_c[...]
         sent["vec_y"] = remote.start(vec_s, vec_y, y_dev)
 
     def vec_along_r():
@@ -827,7 +842,8 @@
         vec_total = vec_q[0]
         for k in away:
             vec_total = vec_total + vec_q[k]
-        vec_out[...] = vec_total
+        vec_out[vec_rows(c), :] = vec_total
+        sent["vec_out"] = remote.start(vec_out.at[vec_rows(c)], vec_out.at[vec_rows(c)], core_dev)
 
     step.update(qv=vec_core, V_y=vec_along_y, V_r=vec_along_r, V_q=vec_along_q, V_e=vec_end)
 
@@ -838,6 +854,7 @@
     mark("finish")
     send_out.wait_recv()
     sent["gtok"].wait_recv()
+    sent["vec_out"].wait_recv()
     remote.finish()
 
 
@@ -1043,14 +1060,14 @@
         pool_fin=V((width, width), F32),
         items=V((2, slots, width), BF16),
         items_c=V((slots, width), BF16),
-        item_all=V((2, n_dp * slots, width), BF16),
+        item_all=V((2, 2, n_dp * slots, width // 2), BF16),
         vec=V((VEC_ROWS, width), F32),
-        vec_c=V((VEC_ROWS, width), F32),
-        vec_s=V((VEC_ROWS, width), F32),
-        vec_y=V((VEC_ROWS, width), F32),
-        vec_t=V((VEC_ROWS, width), F32),
-        vec_r=V((VEC_ROWS, width), F32),
-        vec_q=V((pairs, VEC_ROWS, width), F32),
+        vec_c=V((VEC_ROWS // 2, width), F32),
+        vec_s=V((VEC_ROWS // 2, width), F32),
+        vec_y=V((VEC_ROWS // 2, width), F32),
+        vec_t=V((VEC_ROWS // 2, width), F32),
+        vec_r=V((VEC_ROWS // 2, width), F32),
+        vec_q=V((pairs, VEC_ROWS // 2, width), F32),
         cnt=V((8, 128), F32),
         cnt_y=V((8, 128), F32),
         cnt_s=V((8, 128), F32),

time: 81.9 us -> 78 us (0.952)
  Pallas kernels: 80.9 us -> 77 us
    pallas_call x1, Pallas kernels: 79.2 us -> 75.2 us  [on_device(): pl.pallas_call(partial(layer_kernel, n_dp), out_shape=[V((token_count, wi...]
where the time goes in v4:
time: 78 us; the launch traced here: 77.8 us
  Pallas kernels  77 us (99%)
  between operations  0.83 us (1%)
    pallas_call x1, Pallas kernels, on_device(): pl.pallas_call(partial(layer_kernel, n_dp), out_shape=[V((token_count, wi...  75.2 us
    pallas_call x1, Pallas kernels, on_device(): pl.pallas_call(partial(place_kernel, n_dp), out_shape=outputs, in_specs=[...  1.77 us

profile of v4, /device:TPU:0, one launch (start us, length us, event | category | flops | bytes accessed | tf_op | source)
XLA Modules:
  0.0 77.8 jit_solution(17645540881115427940)
XLA Ops:
  0.7 75.2 %layer.1 = (bf16[512,768]{1,0:T(8,128)(2,1)S(1)}, bf16[512,768]{1,0:T(8,128)(2,1)S(1)}, f32[96,768]{1,0:T(8,128)S(1)}, f32[96,768]{1,0:T(8,128)S(1)}, f32[96,768...) custom-call(bf16[512,768]{1,0:T(8,128)(2,1)} %tok_hbm.1, bf16[512,768]{1,0:T(8,128)(2,1)} %cot_hbm.1, ...), custom_call_target="tpu_custom_call" | custom-call | tf_op jit(solution)/shard_map/layer/pallas_call | solution.py:1077
  75.9 1.8 %place.1 = (bf16[512,768]{1,0:T(8,128)(2,1)}, bf16[512,768]{1,0:T(8,128)(2,1)}, f32[1,1]{1,0:T(1,128)}, f32[1,1]{1,0:T(1,128)}, f32[3,96,192]{2,1,0:T(8,128)}, /...) custom-call(bf16[512,768]{1,0:T(8,128)(2,1)S(1)} %get-tuple-element., ...), custom_call_target="tpu_custom_call" | custom-call | tf_op jit(solution)/shard_map/place/pallas_call | solution.py:1140

commit v5 on v4

--- a/solution.py
+++ b/solution.py
@@ -366,13 +366,11 @@
     q_away[...] = (dot_nt(wt[c, rows_q, :], tok[away_rows, :]) + query_bias).astype(BF16)
     wide_k = jnp.concatenate([wt[c, rows_k, :], jnp.zeros((pad_rows, width), BF16)], axis=0)
     k_pad[c] = dot_nt(tok[...], wide_k).astype(BF16)
-    v_tr[c] = (dot_nt(wt[c, rows_v, :], tok[...]) + bias_cols(1, token_count)).astype(BF16)
-    q_pad[c, 0:local_width, :] = (dot_nt(wt[c, rows_q, :], tok[own_rows, :]) + query_bias).astype(BF16)
-
     pl.semaphore_wait(barrier, len(peers))
     mark("sends")
     send_q = remote.start(q_away, q_pad.at[c, pl.ds(0, local_width)], core_dev)
     send_k = remote.start(k_pad.at[c], k_pad.at[c], core_dev)
+    v_tr[c] = (dot_nt(wt[c, rows_v, :], tok[...]) + bias_cols(1, token_count)).astype(BF16)
     send_v = remote.start(v_tr.at[c], v_tr.at[c], core_dev)
     send_wo = remote.start(wout_hbm, wo.at[c], core_dev)
     send_bias = remote.start(up_bias.at[c], up_bias.at[c], core_dev)
@@ -380,6 +378,8 @@
     send_wdn = remote.start(wdn_hbm, wdn.at[c], core_dev)
     send_cnt_y = remote.start(cnt, cnt_y, y_dev)
     send_wt = remote.start(wqkv_hbm, wt.at[c], core_dev)
+
+    q_pad[c, 0:local_width, :] = (dot_nt(wt[c, rows_q, :], tok[own_rows, :]) + query_bias).astype(BF16)
 
     half_row = lax.broadcasted_iota(jnp.int32, (128, half), 0) < HD
     inv_root = HD ** (-0.5)

time: 78 us -> 78.5 us (level)
  no operation moved by 1% of the time
where the time goes in v5:
time: 78.5 us; the launch traced here: 78.3 us
  Pallas kernels  77.5 us (99%)
  between operations  0.83 us (1%)
    pallas_call x1, Pallas kernels, on_device(): pl.pallas_call(partial(layer_kernel, n_dp), out_shape=[V((token_count, wi...  75.7 us
    pallas_call x1, Pallas kernels, on_device(): pl.pallas_call(partial(place_kernel, n_dp), out_shape=outputs, in_specs=[...  1.77 us

profile of v5, /device:TPU:0, one launch (start us, length us, event | category | flops | bytes accessed | tf_op | source)
XLA Modules:
  0.0 78.3 jit_solution(722149878281552165)
XLA Ops:
  0.7 75.7 %layer.1 = (bf16[512,768]{1,0:T(8,128)(2,1)S(1)}, bf16[512,768]{1,0:T(8,128)(2,1)S(1)}, f32[96,768]{1,0:T(8,128)S(1)}, f32[96,768]{1,0:T(8,128)S(1)}, f32[96,768...) custom-call(bf16[512,768]{1,0:T(8,128)(2,1)} %tok_hbm.1, bf16[512,768]{1,0:T(8,128)(2,1)} %cot_hbm.1, ...), custom_call_target="tpu_custom_call" | custom-call | tf_op jit(solution)/shard_map/layer/pallas_call | solution.py:1077
  76.4 1.8 %place.1 = (bf16[512,768]{1,0:T(8,128)(2,1)}, bf16[512,768]{1,0:T(8,128)(2,1)}, f32[1,1]{1,0:T(1,128)}, f32[1,1]{1,0:T(1,128)}, f32[3,96,192]{2,1,0:T(8,128)}, /...) custom-call(bf16[512,768]{1,0:T(8,128)(2,1)S(1)} %get-tuple-element., ...), custom_call_target="tpu_custom_call" | custom-call | tf_op jit(solution)/shard_map/place/pallas_call | solution.py:1140
